TPU v7x, 32 devices: a whole 2x2x4 slice. The times are simulated.
32 devices in a mesh: dp: 8 (over y, x, core), lat: 4 (over z).
Axes of the slice: x: 2, y: 2, z: 4, core: 2. Of those that a mesh axis runs over, the one named last changes fastest.
Arguments:
- media: bfloat16 [4, 16, 1280, 1024], P(None, 'dp', 'lat'), may hold values from -6 to 6
- latents: bfloat16 [4, 16, 64, 1024], P(None, 'dp', 'lat'), may hold values from -6 to 6
- counts: int32 [4, 16], P(None, 'dp'), may hold values from 1 to 5
- cotangent: bfloat16 [4, 16, 64, 1024], P(None, 'dp', 'lat'), may hold values from -6 to 6
- gain_media: bfloat16 [1024], P('dp'), may hold values from 0.25 to 1.75
- bias_media: bfloat16 [1024], P('dp'), may hold values from -3 to 3
- gain_latent: bfloat16 [1024], P('dp'), may hold values from 0.25 to 1.75
- bias_latent: bfloat16 [1024], P('dp'), may hold values from -3 to 3
- gain_ff: bfloat16 [1024], P('dp'), may hold values from 0.25 to 1.75
- bias_ff: bfloat16 [1024], P('dp'), may hold values from -3 to 3
- w_query: bfloat16 [1024, 512], P('dp'), may hold values from -0.375 to 0.375
- w_keyval: bfloat16 [1024, 1024], P('dp'), may hold values from -0.1875 to 0.1875
- w_out: bfloat16 [512, 1024], P('dp'), may hold values from -1 to 1
- w_up: bfloat16 [1024, 4096], P('dp'), may hold values from -0.1875 to 0.1875
- w_down: bfloat16 [4096, 1024], P('dp'), may hold values from -0.09375 to 0.09375
Outputs:
- latents_out: bfloat16 [4, 16, 64, 1024], P(None, 'dp', 'lat')
- media_grad: bfloat16 [4, 16, 1280, 1024], P(None, 'dp', 'lat')
- latent_grad: bfloat16 [4, 16, 64, 1024], P(None, 'dp', 'lat')
- grad_gain_media: float32 [1024], P('dp')
- grad_bias_media: float32 [1024], P('dp')
- grad_gain_latent: float32 [1024], P('dp')
- grad_bias_latent: float32 [1024], P('dp')
- grad_gain_ff: float32 [1024], P('dp')
- grad_bias_ff: float32 [1024], P('dp')
- grad_query: float32 [1024, 512], P('dp')
- grad_keyval: float32 [1024, 1024], P('dp')
- grad_out: float32 [512, 1024], P('dp')
- grad_up: float32 [1024, 4096], P('dp')
- grad_down: float32 [4096, 1024], P('dp')
Inputs may be any that keep to these rules, and one draw needn't show every extreme that they name: `counts`: number of images of a sample; its media rows from 256 * count on are padding.
All inputs are finite; a program needn't handle non-finite values.
Results may differ from a plain program's by a relative error of at most 0.017.
Values may be sent and summed in bfloat16 or wider, within the bound.
A program may use at most 248 MiB of HBM per device.

v0:
```python
import jax
import jax.numpy as jnp
from jax import lax
from jax.sharding import PartitionSpec as P

HEADS = 8
HEAD = 64
VIS = 256


EPS = 1e-05
F32 = jnp.float32
B16 = jnp.bfloat16


def norm_parts(x, gain, bias):
    mean = jnp.mean(x, -1, keepdims=True)
    cent = x - mean
    factor = lax.rsqrt(jnp.mean(cent * cent, -1, keepdims=True) + EPS)
    unit = cent * factor
    return (unit * gain + bias, unit, factor)


def norm_back(grad, unit, factor, gain):
    scaled = grad * gain
    inner_mean = jnp.mean(scaled * unit, -1, keepdims=True)
    d_input = factor * (scaled - jnp.mean(scaled, -1, keepdims=True) - unit * inner_mean)
    return (d_input, jnp.sum(grad * unit, (0, 1)), jnp.sum(grad, (0, 1)))


def rows_times(left, right):
    return jnp.einsum("sqd,de->sqe", left, right, preferred_element_type=F32)


def times_trans(left, right):
    return jnp.einsum("sqe,de->sqd", left, right, preferred_element_type=F32)


def outer_sum(left, right):
    return jnp.einsum("sqd,sqe->de", left, right, preferred_element_type=F32)


def reduce_each(local):
    shard = (
        lax.psum_scatter(local[0], "dp", scatter_dimension=0, tiled=True),
        lax.psum_scatter(local[1], "dp", scatter_dimension=0, tiled=True),
        lax.psum_scatter(local[2], "dp", scatter_dimension=0, tiled=True),
        lax.psum_scatter(local[3], "dp", scatter_dimension=0, tiled=True),
        lax.psum_scatter(local[4], "dp", scatter_dimension=0, tiled=True),
        lax.psum_scatter(local[5], "dp", scatter_dimension=0, tiled=True),
        lax.psum_scatter(local[6], "dp", scatter_dimension=0, tiled=True),
        lax.psum_scatter(local[7], "dp", scatter_dimension=0, tiled=True),
        lax.psum_scatter(local[8], "dp", scatter_dimension=0, tiled=True),
        lax.psum_scatter(local[9], "dp", scatter_dimension=0, tiled=True),
        lax.psum_scatter(local[10], "dp", scatter_dimension=0, tiled=True),
    )
    return (
        lax.psum(shard[0].astype(jnp.bfloat16), "lat").astype(jnp.float32),
        lax.psum(shard[1].astype(jnp.bfloat16), "lat").astype(jnp.float32),
        lax.psum(shard[2].astype(jnp.bfloat16), "lat").astype(jnp.float32),
        lax.psum(shard[3].astype(jnp.bfloat16), "lat").astype(jnp.float32),
        lax.psum(shard[4].astype(jnp.bfloat16), "lat").astype(jnp.float32),
        lax.psum(shard[5].astype(jnp.bfloat16), "lat").astype(jnp.float32),
        lax.psum(shard[6].astype(jnp.bfloat16), "lat").astype(jnp.float32),
        lax.psum(shard[7].astype(jnp.bfloat16), "lat").astype(jnp.float32),
        lax.psum(shard[8].astype(jnp.bfloat16), "lat").astype(jnp.float32),
        lax.psum(shard[9].astype(jnp.bfloat16), "lat").astype(jnp.float32),
        lax.psum(shard[10].astype(jnp.bfloat16), "lat").astype(jnp.float32),
    )


def shards(
    media,
    latents,
    counts,
    cotangent,
    gain_media,
    bias_media,
    gain_latent,
    bias_latent,
    gain_ff,
    bias_ff,
    w_query,
    w_keyval,
    w_out,
    w_up,
    w_down,
):
    micro_count = media.shape[0]
    outs_list = []
    med_list = []
    lat_list = []
    totals = None
    for micro in range(micro_count):
        whole = (
            lax.all_gather(gain_media, "dp", axis=0, tiled=True),
            lax.all_gather(bias_media, "dp", axis=0, tiled=True),
            lax.all_gather(gain_latent, "dp", axis=0, tiled=True),
            lax.all_gather(bias_latent, "dp", axis=0, tiled=True),
            lax.all_gather(gain_ff, "dp", axis=0, tiled=True),
            lax.all_gather(bias_ff, "dp", axis=0, tiled=True),
            lax.all_gather(w_query, "dp", axis=0, tiled=True),
            lax.all_gather(w_keyval, "dp", axis=0, tiled=True),
            lax.all_gather(w_out, "dp", axis=0, tiled=True),
            lax.all_gather(w_up, "dp", axis=0, tiled=True),
            lax.all_gather(w_down, "dp", axis=0, tiled=True),
        )
        g_med, b_med, g_lat, b_lat, g_ffn, b_ffn, wq_all, wkv_all, wo_all, wup_all, wdown_all = (
            whole
        )
        g_med = g_med.astype(F32)
        b_med = b_med.astype(F32)
        g_lat = g_lat.astype(F32)
        b_lat = b_lat.astype(F32)
        g_ffn = g_ffn.astype(F32)
        b_ffn = b_ffn.astype(F32)
        inner = wq_all.shape[1]
        med_f = media[micro].astype(F32)
        lat_f = latents[micro].astype(F32)
        cot = cotangent[micro]
        counts_now = counts[micro]
        samples = med_f.shape[0]
        q_rows = lat_f.shape[1]
        med_out, med_unit, med_factor = norm_parts(med_f, g_med, b_med)
        med_norm = med_out.astype(B16)
        lat_out, lat_unit, lat_factor = norm_parts(lat_f, g_lat, b_lat)
        lat_norm = lat_out.astype(B16)
        query = (rows_times(lat_norm, wq_all) * 0.125).astype(B16)
        kv_med = rows_times(med_norm, wkv_all).astype(B16)
        kv_lat = rows_times(lat_norm, wkv_all).astype(B16)
        all_med, all_lat = (
            lax.all_gather(kv_med, "lat", axis=1, tiled=True),
            lax.all_gather(kv_lat, "lat", axis=1, tiled=True),
        )
        media_rows = all_med.shape[1]
        keyval = jnp.concatenate([all_med, all_lat], 1)
        key_count = keyval.shape[1]
        keys = keyval[:, :, :inner].reshape(samples, key_count, HEADS, HEAD)
        values = keyval[:, :, inner:].reshape(samples, key_count, HEADS, HEAD)
        heads_q = query.reshape(samples, q_rows, HEADS, HEAD)
        slot_of = lax.iota(jnp.int32, media_rows) // VIS
        live = jnp.concatenate(
            [
                slot_of[None, :] < counts_now[:, None],
                jnp.ones((samples, all_lat.shape[1]), dtype=bool),
            ],
            1,
        )

        def scores_of():
            raw = jnp.einsum("sqhd,skhd->shqk", heads_q, keys, preferred_element_type=F32)
            return jnp.where(live[:, None, None, :], raw, -1e30)

        score = scores_of()
        top = jnp.max(score, -1, keepdims=True)
        log_total = top + jnp.log(jnp.sum(jnp.exp(score - top), -1, keepdims=True))
        prob_low = jnp.exp(score - log_total).astype(B16)
        attended = (
            jnp.einsum("shqk,skhd->sqhd", prob_low, values, preferred_element_type=F32)
            .astype(B16)
            .reshape(samples, q_rows, inner)
        )
        hidden = lat_f + rows_times(attended, wo_all)
        ffn_out, ffn_unit, ffn_factor = norm_parts(hidden, g_ffn, b_ffn)
        ff_norm = ffn_out.astype(B16)
        up = rows_times(ff_norm, wup_all)
        act = jax.nn.gelu(up, approximate=False).astype(B16)
        outs_list.append((hidden + rows_times(act, wdown_all)).astype(B16))
        grad_down = outer_sum(act, cot)
        d_act = times_trans(cot, wdown_all)
        gelu_out, gelu_pull = jax.vjp(lambda v: jax.nn.gelu(v, approximate=False), up)
        d_up = gelu_pull(d_act)[0].astype(B16)
        grad_up = outer_sum(ff_norm, d_up)
        d_ffn = times_trans(d_up, wup_all)
        d_hnorm, grad_gf, grad_bf = norm_back(d_ffn, ffn_unit, ffn_factor, g_ffn)
        d_hidden = cot.astype(F32) + d_hnorm
        d_attn = d_hidden.astype(B16)
        grad_wo = outer_sum(attended, d_attn)
        d_attended = times_trans(d_attn, wo_all).astype(B16).reshape(samples, q_rows, HEADS, HEAD)
        prob = jnp.exp(scores_of() - log_total)
        d_prob = jnp.einsum("sqhd,skhd->shqk", d_attended, values, preferred_element_type=F32)
        spread_sum = jnp.sum(d_prob * prob, -1, keepdims=True)
        d_score = (prob * (d_prob - spread_sum)).astype(B16)
        d_query = jnp.einsum("shqk,skhd->sqhd", d_score, keys, preferred_element_type=F32).astype(
            B16
        )
        d_keys = jnp.einsum(
            "shqk,sqhd->skhd", d_score, heads_q, preferred_element_type=F32
        ).reshape(samples, key_count, inner)
        d_values = jnp.einsum(
            "shqk,sqhd->skhd", prob_low, d_attended, preferred_element_type=F32
        ).reshape(samples, key_count, inner)
        dk_med, dv_med, dk_lat, dv_lat = (
            lax.psum_scatter(
                d_keys[:, :media_rows].astype(jnp.bfloat16), "lat", scatter_dimension=1, tiled=True
            ).astype(jnp.float32),
            lax.psum_scatter(
                d_values[:, :media_rows].astype(jnp.bfloat16),
                "lat",
                scatter_dimension=1,
                tiled=True,
            ).astype(jnp.float32),
            lax.psum_scatter(
                d_keys[:, media_rows:].astype(jnp.bfloat16), "lat", scatter_dimension=1, tiled=True
            ).astype(jnp.float32),
            lax.psum_scatter(
                d_values[:, media_rows:].astype(jnp.bfloat16),
                "lat",
                scatter_dimension=1,
                tiled=True,
            ).astype(jnp.float32),
        )
        dk_med = dk_med.astype(B16)
        dv_med = dv_med.astype(B16)
        dk_lat = dk_lat.astype(B16)
        dv_lat = dv_lat.astype(B16)
        w_key = wkv_all[:, :inner]
        w_val = wkv_all[:, inner:]
        grad_kv = jnp.concatenate(
            [
                outer_sum(med_norm, dk_med) + outer_sum(lat_norm, dk_lat),
                outer_sum(med_norm, dv_med) + outer_sum(lat_norm, dv_lat),
            ],
            1,
        )
        d_mnorm = times_trans(dk_med, w_key) + times_trans(dv_med, w_val)
        d_media, grad_gm, grad_bm = norm_back(d_mnorm, med_unit, med_factor, g_med)
        med_list.append(d_media.astype(B16))
        d_qscaled = (d_query * 0.125).reshape(samples, q_rows, inner)
        grad_wq = outer_sum(lat_norm, d_qscaled)
        d_lnorm = (
            times_trans(d_qscaled, wq_all) + times_trans(dk_lat, w_key) + times_trans(dv_lat, w_val)
        )
        d_latn, grad_gl, grad_bl = norm_back(d_lnorm, lat_unit, lat_factor, g_lat)
        lat_list.append((d_hidden + d_latn).astype(B16))
        local = (
            grad_gm,
            grad_bm,
            grad_gl,
            grad_bl,
            grad_gf,
            grad_bf,
            grad_wq,
            grad_kv,
            grad_wo,
            grad_up,
            grad_down,
        )
        part = reduce_each(local)
        if totals is None:
            totals = part
        else:
            totals = tuple((a + b for a, b in zip(totals, part)))
    return (
        jnp.stack(outs_list, 0),
        jnp.stack(med_list, 0),
        jnp.stack(lat_list, 0),
        totals[0],
        totals[1],
        totals[2],
        totals[3],
        totals[4],
        totals[5],
        totals[6],
        totals[7],
        totals[8],
        totals[9],
        totals[10],
    )


def solution(mesh):
    placed = (
        P(None, "dp", "lat", None),
        P(None, "dp", "lat", None),
        P(None, "dp"),
        P(None, "dp", "lat", None),
        P("dp"),
        P("dp"),
        P("dp"),
        P("dp"),
        P("dp"),
        P("dp"),
        P("dp", None),
        P("dp", None),
        P("dp", None),
        P("dp", None),
        P("dp", None),
    )
    return jax.shard_map(
        shards,
        mesh=mesh,
        in_specs=placed,
        out_specs=(
            P(None, "dp", "lat", None),
            P(None, "dp", "lat", None),
            P(None, "dp", "lat", None),
            P("dp"),
            P("dp"),
            P("dp"),
            P("dp"),
            P("dp"),
            P("dp"),
            P("dp", None),
            P("dp", None),
            P("dp", None),
            P("dp", None),
            P("dp", None),
        ),
        check_vma=False,
    )
```

profile of v0, /device:TPU:0, one launch (start us, length us, event | category | flops | bytes accessed | tf_op | source)
XLA Modules:
  0.0 3246.3 jit_solution(9213537862936248211)
XLA Ops:
  8.7 10.3 all-gather
  19.0 8.6 all-gather.1
  47.1 8.7 all-gather.2
  63.6 8.7 all-gather.4
  85.3 17.8 all_gather.106
  103.1 67.2 %all-gather.30.cloned.1.call-done = bf16[2,1280,1024]{2,1,0:T(8,128)(2,1)} async-done(((bf16[2,320,1024]{2,1,0:T(8,128)(2,1)}), bf16[2,1280,1024]{2,1,0:T(8,128)(2,1)}) %all-gather.30.cloned.1.call-update) | async-done | bytes 5242896 | tf_op jit(solution)/shard_map/all_gather | solution.py:132
  197.0 53.2 %all-gather.24.cloned.1.call-done = bf16[1024,4096]{1,0:T(8,128)(2,1)} async-done(((bf16[128,4096]{1,0:T(8,128)(2,1)}), bf16[1024,4096]{1,0:T(8,128)(2,1)}) %all-gather.24.cloned.1.call-update) | async-done | bytes 8388624 | tf_op jit(solution)/shard_map/all_gather | solution.py:105
  256.9 49.5 %all-gather.26.cloned.1.call-done = bf16[4096,1024]{1,0:T(8,128)(2,1)} async-done(((bf16[512,1024]{1,0:T(8,128)(2,1)}), bf16[4096,1024]{1,0:T(8,128)(2,1)}) %all-gather.26.cloned.1.call-update) | async-done | bytes 8388624 | tf_op jit(solution)/shard_map/all_gather | solution.py:106
  347.1 38.2 %reduce-scatter.45.cloned.1.call-done = bf16[2,320,512]{2,1,0:T(8,128)(2,1)} async-done(((bf16[2,1280,512]{2,1,0:T(8,128)(2,1)}), bf16[2,320,512]{2,1,0:T(8,128)(2,1)}) %reduce-scatter.45.cloned.1.call-update) | async-done | bytes 655376 | tf_op jit(solution)/shard_map/reduce_scatter | solution.py:194
  388.8 50.7 %reduce-scatter.47.cloned.1.call-done = bf16[2,320,512]{2,1,0:T(8,128)(2,1)} async-done(((bf16[2,1280,512]{2,1,0:T(8,128)(2,1)}), bf16[2,320,512]{2,1,0:T(8,128)(2,1)}) %reduce-scatter.47.cloned.1.call-update) | async-done | bytes 655376 | tf_op jit(solution)/shard_map/reduce_scatter | solution.py:197
  468.0 13.4 reduce-scatter.63.cloned.1.call-done
  492.6 15.8 all_gather.104
  508.9 18.4 all_gather.44
  527.8 18.9 all_gather.108
  546.7 45.1 %all-gather.32.cloned.1.call-done = bf16[2,1280,1024]{2,1,0:T(8,128)(2,1)} async-done(((bf16[2,320,1024]{2,1,0:T(8,128)(2,1)}), bf16[2,1280,1024]{2,1,0:T(8,128)(2,1)}) %all-gather.32.cloned.1.call-update) | async-done | bytes 5242896 | tf_op jit(solution)/shard_map/all_gather | solution.py:132
  599.8 90.3 %all-gather.18.cloned.1.call-done = bf16[2,1280,1024]{2,1,0:T(8,128)(2,1)} async-done(((bf16[2,320,1024]{2,1,0:T(8,128)(2,1)}), bf16[2,1280,1024]{2,1,0:T(8,128)(2,1)}) %all-gather.18.cloned.1.call-update) | async-done | bytes 5242896 | tf_op jit(solution)/shard_map/all_gather | solution.py:132
  698.1 90.7 %all-gather.28.cloned.1.call-done = bf16[2,1280,1024]{2,1,0:T(8,128)(2,1)} async-done(((bf16[2,320,1024]{2,1,0:T(8,128)(2,1)}), bf16[2,1280,1024]{2,1,0:T(8,128)(2,1)}) %all-gather.28.cloned.1.call-update) | async-done | bytes 5242896 | tf_op jit(solution)/shard_map/all_gather | solution.py:132
  1005.9 17.4 reduce-scatter.57.cloned.1.call-done
  1028.4 47.4 %reduce-scatter.51.cloned.1.call-done = bf16[2,320,512]{2,1,0:T(8,128)(2,1)} async-done(((bf16[2,1280,512]{2,1,0:T(8,128)(2,1)}), bf16[2,320,512]{2,1,0:T(8,128)(2,1)}) %reduce-scatter.51.cloned.1.call-update) | async-done | bytes 655376 | tf_op jit(solution)/shard_map/reduce_scatter | solution.py:197
  1079.7 50.1 %reduce-scatter.49.cloned.1.call-done = bf16[2,320,512]{2,1,0:T(8,128)(2,1)} async-done(((bf16[2,1280,512]{2,1,0:T(8,128)(2,1)}), bf16[2,320,512]{2,1,0:T(8,128)(2,1)}) %reduce-scatter.49.cloned.1.call-update) | async-done | bytes 655376 | tf_op jit(solution)/shard_map/reduce_scatter | solution.py:194
  1133.9 16.9 reduce-scatter.67.cloned.1.call-done
  1152.9 17.7 reduce-scatter.65.cloned.1.call-done
  1175.3 47.8 %reduce-scatter.39.cloned.1.call-done = bf16[2,320,512]{2,1,0:T(8,128)(2,1)} async-done(((bf16[2,1280,512]{2,1,0:T(8,128)(2,1)}), bf16[2,320,512]{2,1,0:T(8,128)(2,1)}) %reduce-scatter.39.cloned.1.call-update) | async-done | bytes 655376 | tf_op jit(solution)/shard_map/reduce_scatter | solution.py:197
  1227.2 50.1 %reduce-scatter.37.cloned.1.call-done = bf16[2,320,512]{2,1,0:T(8,128)(2,1)} async-done(((bf16[2,1280,512]{2,1,0:T(8,128)(2,1)}), bf16[2,320,512]{2,1,0:T(8,128)(2,1)}) %reduce-scatter.37.cloned.1.call-update) | async-done | bytes 655376 | tf_op jit(solution)/shard_map/reduce_scatter | solution.py:194
  1281.3 16.9 reduce-scatter.55.cloned.1.call-done
  1300.3 17.6 reduce-scatter.53.cloned.1.call-done
  1323.7 9.1 convolution_bitcast_fusion.1
  1411.7 48.8 %reduce-scatter.81.cloned.1.call-done = f32[128,1024]{0,1:T(8,128)} async-done(((f32[1024,1024]{0,1:T(8,128)}), f32[128,1024]{0,1:T(8,128)}) %reduce-scatter.81.cloned.1.call-update) | async-done | bytes 524304 | tf_op jit(solution)/shard_map/reduce_scatter | solution.py:52
  1479.0 26.3 reduce-scatter.69.cloned.1.call-done
  1507.0 43.3 %reduce-scatter.75.cloned.1.call-done = f32[128,512]{1,0:T(8,128)} async-done(((f32[1024,512]{1,0:T(8,128)}), f32[128,512]{1,0:T(8,128)}) %reduce-scatter.75.cloned.1.call-update) | async-done | bytes 262160 | tf_op jit(solution)/shard_map/reduce_scatter | solution.py:51
  1551.9 43.3 %reduce-scatter.71.cloned.1.call-done = f32[128,512]{1,0:T(8,128)} async-done(((f32[1024,512]{1,0:T(8,128)}), f32[128,512]{1,0:T(8,128)}) %reduce-scatter.71.cloned.1.call-update) | async-done | bytes 262160 | tf_op jit(solution)/shard_map/reduce_scatter | solution.py:51
  1596.8 42.9 %reduce-scatter.85.cloned.1.call-done = f32[64,1024]{1,0:T(8,128)} async-done(((f32[512,1024]{1,0:T(8,128)}), f32[64,1024]{1,0:T(8,128)}) %reduce-scatter.85.cloned.1.call-update) | async-done | bytes 262160 | tf_op jit(solution)/shard_map/reduce_scatter | solution.py:53
  1641.3 43.1 %reduce-scatter.87.cloned.1.call-done = f32[64,1024]{1,0:T(8,128)} async-done(((f32[512,1024]{1,0:T(8,128)}), f32[64,1024]{1,0:T(8,128)}) %reduce-scatter.87.cloned.1.call-update) | async-done | bytes 262160 | tf_op jit(solution)/shard_map/reduce_scatter | solution.py:53
  1686.1 42.9 %reduce-scatter.91.cloned.1.call-done = f32[64,1024]{1,0:T(8,128)} async-done(((f32[512,1024]{1,0:T(8,128)}), f32[64,1024]{1,0:T(8,128)}) %reduce-scatter.91.cloned.1.call-update) | async-done | bytes 262160 | tf_op jit(solution)/shard_map/reduce_scatter | solution.py:53
  1730.6 53.5 %reduce-scatter.79.cloned.1.call-done = f32[128,1024]{0,1:T(8,128)} async-done(((f32[1024,1024]{0,1:T(8,128)}), f32[128,1024]{0,1:T(8,128)}) %reduce-scatter.79.cloned.1.call-update) | async-done | bytes 524304 | tf_op jit(solution)/shard_map/reduce_scatter | solution.py:52
  1785.9 53.3 %reduce-scatter.83.cloned.1.call-done = f32[128,1024]{0,1:T(8,128)} async-done(((f32[1024,1024]{0,1:T(8,128)}), f32[128,1024]{0,1:T(8,128)}) %reduce-scatter.83.cloned.1.call-update) | async-done | bytes 524304 | tf_op jit(solution)/shard_map/reduce_scatter | solution.py:52
  1841.0 53.2 %reduce-scatter.77.cloned.1.call-done = f32[128,1024]{0,1:T(8,128)} async-done(((f32[1024,1024]{0,1:T(8,128)}), f32[128,1024]{0,1:T(8,128)}) %reduce-scatter.77.cloned.1.call-update) | async-done | bytes 524304 | tf_op jit(solution)/shard_map/reduce_scatter | solution.py:52
  1895.9 117.8 %reduce-scatter.105.cloned.1.call-done = f32[512,1024]{1,0:T(8,128)} async-done(((f32[4096,1024]{1,0:T(8,128)}), f32[512,1024]{1,0:T(8,128)}) %reduce-scatter.105.cloned.1.call-update) | async-done | bytes 2097168 | tf_op jit(solution)/shard_map/reduce_scatter | solution.py:55
  2016.5 116.7 %reduce-scatter.97.cloned.1.call-done = f32[128,4096]{1,0:T(8,128)} async-done(((f32[1024,4096]{1,0:T(8,128)}), f32[128,4096]{1,0:T(8,128)}) %reduce-scatter.97.cloned.1.call-update) | async-done | bytes 2097168 | tf_op jit(solution)/shard_map/reduce_scatter | solution.py:54
  2135.9 116.9 %reduce-scatter.107.cloned.1.call-done = f32[512,1024]{1,0:T(8,128)} async-done(((f32[4096,1024]{1,0:T(8,128)}), f32[512,1024]{1,0:T(8,128)}) %reduce-scatter.107.cloned.1.call-update) | async-done | bytes 2097168 | tf_op jit(solution)/shard_map/reduce_scatter | solution.py:55
  2255.5 116.8 %reduce-scatter.101.cloned.1.call-done = f32[512,1024]{1,0:T(8,128)} async-done(((f32[4096,1024]{1,0:T(8,128)}), f32[512,1024]{1,0:T(8,128)}) %reduce-scatter.101.cloned.1.call-update) | async-done | bytes 2097168 | tf_op jit(solution)/shard_map/reduce_scatter | solution.py:55
  2375.0 116.8 %reduce-scatter.103.cloned.1.call-done = f32[512,1024]{1,0:T(8,128)} async-done(((f32[4096,1024]{1,0:T(8,128)}), f32[512,1024]{1,0:T(8,128)}) %reduce-scatter.103.cloned.1.call-update) | async-done | bytes 2097168 | tf_op jit(solution)/shard_map/reduce_scatter | solution.py:55
  2494.6 116.7 %reduce-scatter.93.cloned.1.call-done = f32[128,4096]{1,0:T(8,128)} async-done(((f32[1024,4096]{1,0:T(8,128)}), f32[128,4096]{1,0:T(8,128)}) %reduce-scatter.93.cloned.1.call-update) | async-done | bytes 2097168 | tf_op jit(solution)/shard_map/reduce_scatter | solution.py:54
  2614.0 116.9 %reduce-scatter.99.cloned.1.call-done = f32[128,4096]{1,0:T(8,128)} async-done(((f32[1024,4096]{1,0:T(8,128)}), f32[128,4096]{1,0:T(8,128)}) %reduce-scatter.99.cloned.1.call-update) | async-done | bytes 2097168 | tf_op jit(solution)/shard_map/reduce_scatter | solution.py:54
  2733.6 116.7 %reduce-scatter.95.cloned.1.call-done = f32[128,4096]{1,0:T(8,128)} async-done(((f32[1024,4096]{1,0:T(8,128)}), f32[128,4096]{1,0:T(8,128)}) %reduce-scatter.95.cloned.1.call-update) | async-done | bytes 2097168 | tf_op jit(solution)/shard_map/reduce_scatter | solution.py:54
  2873.5 25.9 all-reduce.28
  2901.2 19.6 all-reduce.29
  2935.6 292.9 %all-reduce.33.cloned.1.call-done = (bf16[128,512]{1,0:T(8,128)(2,1)}, bf16[128,512]{1,0:T(8,128)(2,1)}, bf16[128,512]{1,0:T(8,128)(2,1)}, bf16[128,512]{1,0:T(8...) async-done(((bf16[128,512]{1,0:T(8,128)(2,1)}, ...) | async-done | bytes 10485776 | tf_op jit(solution)/shard_map/psum | solution.py:64
  (1014 shorter events, 606.8 us)
Async XLA Ops:
  7.2 33.4 %all-gather.16.cloned.1.call-start = ((), (), s32[]{:S(2)}) async-start(), calls=%async_computation.36 | async-start | bytes 2359296 | tf_op jit(solution)/shard_map/all_gather | solution.py:103
  7.9 74.6 %all-gather.20.cloned.1.call-start = ((), (), s32[]{:S(2)}) async-start(), calls=%async_computation.38 | async-start | bytes 1179648 | tf_op jit(solution)/shard_map/all_gather | solution.py:102
  8.7 161.7 %all-gather.30.cloned.1.call-start = ((), (), s32[]{:S(2)}) async-start(), calls=%async_computation.43 | async-start | bytes 6553600 | tf_op jit(solution)/shard_map/all_gather | solution.py:132
  45.3 148.7 %all-gather.22.cloned.1.call-start = ((), (), s32[]{:S(2)}) async-start(), calls=%async_computation.39 | async-start | bytes 1179648 | tf_op jit(solution)/shard_map/all_gather | solution.py:104
  45.9 204.4 %all-gather.24.cloned.1.call-start = ((), (), s32[]{:S(2)}) async-start(), calls=%async_computation.40 | async-start | bytes 9437184 | tf_op jit(solution)/shard_map/all_gather | solution.py:105
  46.4 259.9 %all-gather.26.cloned.1.call-start = ((), (), s32[]{:S(2)}) async-start(), calls=%async_computation.41 | async-start | bytes 9437184 | tf_op jit(solution)/shard_map/all_gather | solution.py:106
  47.0 338.3 %reduce-scatter.45.cloned.1.call-start = ((), (), s32[]{:S(2)}) async-start(), calls=%async_computation.49 | async-start | bytes 3276800 | tf_op jit(solution)/shard_map/reduce_scatter | solution.py:194
  333.1 106.4 %reduce-scatter.47.cloned.1.call-start = ((), (), s32[]{:S(2)}) async-start(), calls=%async_computation.50 | async-start | bytes 3276800 | tf_op jit(solution)/shard_map/reduce_scatter | solution.py:197
  343.3 122.8 %reduce-scatter.61.cloned.1.call-start = ((), (), s32[]{:S(2)}) async-start(), calls=%async_computation.57 | async-start | bytes 163840 | tf_op jit(solution)/shard_map/reduce_scatter | solution.py:203
  345.1 136.3 %reduce-scatter.63.cloned.1.call-start = ((), (), s32[]{:S(2)}) async-start(), calls=%async_computation.58 | async-start | bytes 163840 | tf_op jit(solution)/shard_map/reduce_scatter | solution.py:206
  347.1 244.7 %all-gather.32.cloned.1.call-start = ((), (), s32[]{:S(2)}) async-start(), calls=%async_computation.44 | async-start | bytes 6553600 | tf_op jit(solution)/shard_map/all_gather | solution.py:132
  449.9 240.2 %all-gather.18.cloned.1.call-start = ((), (), s32[]{:S(2)}) async-start(), calls=%async_computation.37 | async-start | bytes 6553600 | tf_op jit(solution)/shard_map/all_gather | solution.py:132
  454.1 334.7 %all-gather.28.cloned.1.call-start = ((), (), s32[]{:S(2)}) async-start(), calls=%async_computation.42 | async-start | bytes 6553600 | tf_op jit(solution)/shard_map/all_gather | solution.py:132
  458.2 529.4 %reduce-scatter.43.cloned.1.call-start = ((), (), s32[]{:S(2)}) async-start(), calls=%async_computation.48 | async-start | bytes 3276800 | tf_op jit(solution)/shard_map/reduce_scatter | solution.py:197
  485.1 317.5 %copy-start.77 = (bf16[2,16,8,64]{3,2,1,0:T(8,128)(2,1)}, bf16[2,16,8,64]{3,2,1,0:T(8,128)(2,1)S(1)}, u32[]{:S(2)}) copy-start(bf16[2,16,8,64]{3,2,1,0:T(8,128)(2,1)S(1)} %reshape.452) | copy-start | bytes 98308
  487.6 312.2 %copy-start.75 = (bf16[2,16,8,64]{3,2,1,0:T(8,128)(2,1)}, bf16[2,16,8,64]{3,2,1,0:T(8,128)(2,1)S(1)}, u32[]{:S(2)}) copy-start(bf16[2,16,8,64]{3,2,1,0:T(8,128)(2,1)S(1)} %reshape.440) | copy-start | bytes 98308
  878.1 113.5 %reduce-scatter.41.cloned.1.call-start = ((), (), s32[]{:S(2)}) async-start(), calls=%async_computation.47 | async-start | bytes 3276800 | tf_op jit(solution)/shard_map/reduce_scatter | solution.py:194
  891.8 112.0 %reduce-scatter.59.cloned.1.call-start = ((), (), s32[]{:S(2)}) async-start(), calls=%async_computation.56 | async-start | bytes 163840 | tf_op jit(solution)/shard_map/reduce_scatter | solution.py:206
  895.3 128.0 %reduce-scatter.57.cloned.1.call-start = ((), (), s32[]{:S(2)}) async-start(), calls=%async_computation.55 | async-start | bytes 163840 | tf_op jit(solution)/shard_map/reduce_scatter | solution.py:203
  899.3 176.5 %reduce-scatter.51.cloned.1.call-start = ((), (), s32[]{:S(2)}) async-start(), calls=%async_computation.52 | async-start | bytes 3276800 | tf_op jit(solution)/shard_map/reduce_scatter | solution.py:197
  909.4 220.4 %reduce-scatter.49.cloned.1.call-start = ((), (), s32[]{:S(2)}) async-start(), calls=%async_computation.51 | async-start | bytes 3276800 | tf_op jit(solution)/shard_map/reduce_scatter | solution.py:194
  922.4 228.3 %reduce-scatter.67.cloned.1.call-start = ((), (), s32[]{:S(2)}) async-start(), calls=%async_computation.60 | async-start | bytes 163840 | tf_op jit(solution)/shard_map/reduce_scatter | solution.py:206
  924.3 246.3 %reduce-scatter.65.cloned.1.call-start = ((), (), s32[]{:S(2)}) async-start(), calls=%async_computation.59 | async-start | bytes 163840 | tf_op jit(solution)/shard_map/reduce_scatter | solution.py:203
  927.7 295.5 %reduce-scatter.39.cloned.1.call-start = ((), (), s32[]{:S(2)}) async-start(), calls=%async_computation.46 | async-start | bytes 3276800 | tf_op jit(solution)/shard_map/reduce_scatter | solution.py:197
  936.4 340.9 %reduce-scatter.37.cloned.1.call-start = ((), (), s32[]{:S(2)}) async-start(), calls=%async_computation.45 | async-start | bytes 3276800 | tf_op jit(solution)/shard_map/reduce_scatter | solution.py:194
  947.4 350.8 %reduce-scatter.55.cloned.1.call-start = ((), (), s32[]{:S(2)}) async-start(), calls=%async_computation.54 | async-start | bytes 163840 | tf_op jit(solution)/shard_map/reduce_scatter | solution.py:206
  950.9 367.1 %reduce-scatter.53.cloned.1.call-start = ((), (), s32[]{:S(2)}) async-start(), calls=%async_computation.53 | async-start | bytes 163840 | tf_op jit(solution)/shard_map/reduce_scatter | solution.py:203
  953.4 454.4 %reduce-scatter.73.cloned.1.call-start = ((), (), s32[]{:S(2)}) async-start(), calls=%async_computation.63 | async-start | bytes 2359296 | tf_op jit(solution)/shard_map/reduce_scatter | solution.py:51
  955.4 454.1 %reduce-scatter.89.cloned.1.call-start = ((), (), s32[]{:S(2)}) async-start(), calls=%async_computation.71 | async-start | bytes 2359296 | tf_op jit(solution)/shard_map/reduce_scatter | solution.py:53
  957.3 503.2 %reduce-scatter.81.cloned.1.call-start = ((), (), s32[]{:S(2)}) async-start(), calls=%async_computation.67 | async-start | bytes 4718592 | tf_op jit(solution)/shard_map/reduce_scatter | solution.py:52
  966.5 538.8 %reduce-scatter.69.cloned.1.call-start = ((), (), s32[]{:S(2)}) async-start(), calls=%async_computation.61 | async-start | bytes 2359296 | tf_op jit(solution)/shard_map/reduce_scatter | solution.py:51
  972.4 577.9 %reduce-scatter.75.cloned.1.call-start = ((), (), s32[]{:S(2)}) async-start(), calls=%async_computation.64 | async-start | bytes 2359296 | tf_op jit(solution)/shard_map/reduce_scatter | solution.py:51
  976.7 618.5 %reduce-scatter.71.cloned.1.call-start = ((), (), s32[]{:S(2)}) async-start(), calls=%async_computation.62 | async-start | bytes 2359296 | tf_op jit(solution)/shard_map/reduce_scatter | solution.py:51
  981.9 657.8 %reduce-scatter.85.cloned.1.call-start = ((), (), s32[]{:S(2)}) async-start(), calls=%async_computation.69 | async-start | bytes 2359296 | tf_op jit(solution)/shard_map/reduce_scatter | solution.py:53
  983.7 700.7 %reduce-scatter.87.cloned.1.call-start = ((), (), s32[]{:S(2)}) async-start(), calls=%async_computation.70 | async-start | bytes 2359296 | tf_op jit(solution)/shard_map/reduce_scatter | solution.py:53
  985.6 743.3 %reduce-scatter.91.cloned.1.call-start = ((), (), s32[]{:S(2)}) async-start(), calls=%async_computation.72 | async-start | bytes 2359296 | tf_op jit(solution)/shard_map/reduce_scatter | solution.py:53
  987.5 796.6 %reduce-scatter.79.cloned.1.call-start = ((), (), s32[]{:S(2)}) async-start(), calls=%async_computation.66 | async-start | bytes 4718592 | tf_op jit(solution)/shard_map/reduce_scatter | solution.py:52
  1027.9 811.3 %reduce-scatter.83.cloned.1.call-start = ((), (), s32[]{:S(2)}) async-start(), calls=%async_computation.68 | async-start | bytes 4718592 | tf_op jit(solution)/shard_map/reduce_scatter | solution.py:52
  1175.3 718.9 %reduce-scatter.77.cloned.1.call-start = ((), (), s32[]{:S(2)}) async-start(), calls=%async_computation.65 | async-start | bytes 4718592 | tf_op jit(solution)/shard_map/reduce_scatter | solution.py:52
  1322.6 691.1 %reduce-scatter.105.cloned.1.call-start = ((), (), s32[]{:S(2)}) async-start(), calls=%async_computation.79 | async-start | bytes 18874368 | tf_op jit(solution)/shard_map/reduce_scatter | solution.py:55
  1332.9 800.3 %reduce-scatter.97.cloned.1.call-start = ((), (), s32[]{:S(2)}) async-start(), calls=%async_computation.75 | async-start | bytes 18874368 | tf_op jit(solution)/shard_map/reduce_scatter | solution.py:54
  1342.2 910.5 %reduce-scatter.107.cloned.1.call-start = ((), (), s32[]{:S(2)}) async-start(), calls=%async_computation.80 | async-start | bytes 18874368 | tf_op jit(solution)/shard_map/reduce_scatter | solution.py:55
  1351.8 1020.4 %reduce-scatter.101.cloned.1.call-start = ((), (), s32[]{:S(2)}) async-start(), calls=%async_computation.77 | async-start | bytes 18874368 | tf_op jit(solution)/shard_map/reduce_scatter | solution.py:55
  1361.5 1130.4 %reduce-scatter.103.cloned.1.call-start = ((), (), s32[]{:S(2)}) async-start(), calls=%async_computation.78 | async-start | bytes 18874368 | tf_op jit(solution)/shard_map/reduce_scatter | solution.py:55
  1371.0 1240.3 %reduce-scatter.93.cloned.1.call-start = ((), (), s32[]{:S(2)}) async-start(), calls=%async_computation.73 | async-start | bytes 18874368 | tf_op jit(solution)/shard_map/reduce_scatter | solution.py:54
  1380.4 1350.5 %reduce-scatter.99.cloned.1.call-start = ((), (), s32[]{:S(2)}) async-start(), calls=%async_computation.76 | async-start | bytes 18874368 | tf_op jit(solution)/shard_map/reduce_scatter | solution.py:54
  1389.7 1460.6 %reduce-scatter.95.cloned.1.call-start = ((), (), s32[]{:S(2)}) async-start(), calls=%async_computation.74 | async-start | bytes 18874368 | tf_op jit(solution)/shard_map/reduce_scatter | solution.py:54
  1398.9 1829.7 %all-reduce.33.cloned.1.call-start = ((), (), s32[]{:S(2)}) async-start(), calls=%async_computation.81 | async-start | bytes 20971520 | tf_op jit(solution)/shard_map/psum | solution.py:64
  (284 other events, 3313.9 us)
Sparse Core Ops, SparseCore 0:
  9.9 30.5 all-gather.15
  42.4 23.4 all-gather.19
  68.1 102.1 all-gather.29
  172.1 21.8 all-gather.21
  195.8 54.4 all-gather.23
  252.0 54.3 all-gather.25
  333.2 52.0 reduce-scatter.44
  387.7 51.7 reduce-scatter.46
  442.3 18.8 reduce-scatter.60
  464.0 17.3 reduce-scatter.62
  483.5 108.2 all-gather.31
  593.2 96.8 all-gather.17
  692.3 96.4 all-gather.27
  878.2 50.4 reduce-scatter.42
  930.9 51.7 reduce-scatter.40
  984.8 18.8 reduce-scatter.58
  1005.9 17.2 reduce-scatter.56
  1025.4 50.2 reduce-scatter.50
  1078.0 51.7 reduce-scatter.48
  1132.0 18.7 reduce-scatter.66
  1153.1 17.4 reduce-scatter.64
  1172.9 50.1 reduce-scatter.38
  1225.4 51.7 reduce-scatter.36
  1279.4 18.7 reduce-scatter.54
  1300.5 17.3 reduce-scatter.52
  1321.7 39.2 reduce-scatter.72
  1364.5 41.2 reduce-scatter.88
  1409.1 51.3 reduce-scatter.80
  1464.1 41.2 reduce-scatter.68
  1509.1 41.1 reduce-scatter.74
  1553.9 41.2 reduce-scatter.70
  1598.5 41.1 reduce-scatter.84
  1643.2 41.2 reduce-scatter.86
  1687.7 41.1 reduce-scatter.90
  1732.7 51.3 reduce-scatter.78
  1787.9 51.2 reduce-scatter.82
  1842.8 51.3 reduce-scatter.76
  1897.7 115.9 reduce-scatter.104
  2017.1 115.9 reduce-scatter.96
  2136.7 115.9 reduce-scatter.106
  2256.3 115.9 reduce-scatter.100
  2375.8 115.9 reduce-scatter.102
  2495.3 115.9 reduce-scatter.92
  2614.9 115.9 reduce-scatter.98
  2734.3 115.9 reduce-scatter.94
  2856.0 372.5 all-reduce.32
where the time goes:
time: 3260 us; the launch traced here: 3250 us
  waiting for transfers between devices  2480 us (76%)
  matrix products  305 us (9%)
  local copies, waits for them, and re-layouts  176 us (5%)
  blocking collectives  168 us (5%)
  other arithmetic  94.7 us (3%)
    reduce_scatter x4, waiting for transfers between devices, reduce_each(): lax.psum_scatter(local[10], 'dp', scatter_dimension=0, tiled=True)  468 us
    reduce_scatter x4, waiting for transfers between devices, reduce_each(): lax.psum_scatter(local[9], 'dp', scatter_dimension=0, tiled=True)  467 us
    all_gather x4, waiting for transfers between devices, shards(): lax.all_gather(kv_med, 'lat', axis=1, tiled=True)  293 us
    psum x1, waiting for transfers between devices, reduce_each(): lax.psum(shard[6].astype(jnp.bfloat16), 'lat').astype(jnp.float32)  293 us
    reduce_scatter x4, waiting for transfers between devices, reduce_each(): lax.psum_scatter(local[7], 'dp', scatter_dimension=0, tiled=True)  209 us
    reduce_scatter x4, waiting for transfers between devices, shards(): lax.psum_scatter(d_values[:, :media_rows].astype(jnp.bfloat16), 'lat', sc...  146 us
    reduce_scatter x4, waiting for transfers between devices, shards(): lax.psum_scatter(d_keys[:, :media_rows].astype(jnp.bfloat16), 'lat', scat...  139 us
    reduce_scatter x4, waiting for transfers between devices, reduce_each(): lax.psum_scatter(local[8], 'dp', scatter_dimension=0, tiled=True)  129 us
  transfers between devices with their start and end apart: 46, of which 40 were waited for; matrix products, arithmetic and copies ran while one was open for 13% of the time, Pallas kernels for 0%

commit v1 on v0

v1 whole, which is shorter than its diff:
```python
import functools

import jax
import jax.numpy as jnp
from jax import lax
from jax.experimental import pallas as pl
from jax.experimental.pallas import tpu as pltpu
from jax.sharding import PartitionSpec as P

HEADS = 8
HEAD = 64
VIS = 256
EPS = 1e-05
F32 = jnp.float32
B16 = jnp.bfloat16
MESH = pl.DeviceIdType.MESH
DMA = pltpu.SemaphoreType.DMA


def exchange_kernel(axis, n, modes, *refs):
    count = len(modes)
    ins, outs = refs[:count], refs[count : 2 * count]
    send, recv, own = refs[2 * count :]
    me = lax.axis_index(axis)
    barrier = pltpu.get_barrier_semaphore()
    for k in range(1, n):
        pl.semaphore_signal(
            barrier, inc=1, device_id={axis: lax.rem(me + k, n)}, device_id_type=MESH
        )
    pl.semaphore_wait(barrier, n - 1)
    copies = []
    for k in range(1, n):
        peer = lax.rem(me + k, n)
        for i in range(count):
            source = ins[i] if modes[i] == "gather" else ins[i].at[peer]
            copy = pltpu.make_async_remote_copy(
                source,
                outs[i].at[me],
                send.at[i, k],
                recv.at[i, k],
                device_id={axis: peer},
                device_id_type=MESH,
            )
            copy.start()
            copies.append(copy)
    for i in range(count):
        source = ins[i] if modes[i] == "gather" else ins[i].at[me]
        copy = pltpu.make_async_copy(source, outs[i].at[me], own.at[i])
        copy.start()
        copies.append(copy)
    for copy in copies:
        copy.wait()


class Exchanges:
    def __init__(self, sizes):
        self.sizes = sizes
        self.used = 0

    def __call__(self, axis, arrays, modes):
        n = self.sizes[axis]
        count = len(arrays)
        outs = [
            jax.ShapeDtypeStruct(((n,) + a.shape) if m == "gather" else a.shape, a.dtype)
            for a, m in zip(arrays, modes)
        ]
        self.used += 1
        space = pl.BlockSpec(memory_space=pl.ANY)
        return pl.pallas_call(
            functools.partial(exchange_kernel, axis, n, modes),
            out_shape=outs,
            in_specs=[space] * count,
            out_specs=[space] * count,
            scratch_shapes=[DMA((count, n)), DMA((count, n)), DMA((count,))],
            compiler_params=pltpu.CompilerParams(collective_id=self.used, has_side_effects=True),
            name="exchange_%d" % self.used,
        )(*arrays)


def norm_parts(x):
    mean = jnp.mean(x, -1, keepdims=True)
    cent = x - mean
    factor = lax.rsqrt(jnp.mean(cent * cent, -1, keepdims=True) + EPS)
    return cent * factor, factor


def norm_back(grad, unit, factor, gain):
    scaled = grad * gain
    inner = jnp.mean(scaled * unit, -1, keepdims=True)
    d_input = factor * (scaled - jnp.mean(scaled, -1, keepdims=True) - unit * inner)
    return d_input, jnp.sum(grad * unit, 0), jnp.sum(grad, 0)


def mm(a, b):
    return lax.dot_general(a, b, (((1,), (0,)), ((), ())), preferred_element_type=F32)


def mm_nt(a, b):
    return lax.dot_general(a, b, (((1,), (1,)), ((), ())), preferred_element_type=F32)


def mm_tn(a, b):
    return lax.dot_general(a, b, (((0,), (0,)), ((), ())), preferred_element_type=F32)


def shards(n_dp, n_lat, media, latents, counts, cotangent, g_m, b_m, g_l, b_l, g_f, b_f, wq, wkv, wo, wup, wdown):
    ex = Exchanges({"dp": n_dp, "lat": n_lat})
    micro, per, rows, width = media.shape
    nq = latents.shape[2]
    S = micro * per
    inner = wq.shape[1]
    ff = wup.shape[1]
    ff_part = ff // n_dp
    d_part = width // n_dp
    lat_at = lax.axis_index("lat")
    med = media.reshape(S * rows, width)
    lat = latents.reshape(S * nq, width).astype(F32)
    cot = cotangent.reshape(S * nq, width)
    count = counts.reshape(S)

    small = jnp.stack([g_m, b_m, g_l, b_l, g_f, b_f], 0)
    small_all, wq_all, wkv_all, wo_all = ex("dp", [small, wq, wkv, wo], ["gather"] * 4)
    params = jnp.transpose(small_all, (1, 0, 2)).reshape(6, width).astype(F32)
    wq_all = wq_all.reshape(width, inner)
    wkv_all = wkv_all.reshape(width, 2 * inner)
    wo_all = wo_all.reshape(inner, width)
    wup_cols = jnp.transpose(wup.reshape(d_part, n_dp, ff_part), (1, 0, 2))
    cot_all, wup_s = ex("dp", [cot, wup_cols], ["gather", "swap"])
    cot_all = cot_all.reshape(-1, width)
    wup_s = wup_s.reshape(width, ff_part)

    med_unit, med_factor = norm_parts(med.astype(F32))
    med_norm = (med_unit * params[0] + params[1]).astype(B16)
    lat_unit, lat_factor = norm_parts(lat)
    lat_norm = (lat_unit * params[2] + params[3]).astype(B16)
    query = (mm(lat_norm, wq_all) * 0.125).astype(B16)
    (query_all,) = ex("lat", [query], ["gather"])
    kv_med = mm(med_norm, wkv_all).astype(B16)
    kv_lat = mm(lat_norm, wkv_all).astype(B16)
    keyval = jnp.concatenate(
        [kv_med.reshape(S, rows, 2 * inner), kv_lat.reshape(S, nq, 2 * inner)], 1
    )
    kc = rows + nq
    keys = keyval[:, :, :inner].reshape(S, kc, HEADS, HEAD)
    values = keyval[:, :, inner:].reshape(S, kc, HEADS, HEAD)
    heads_q = query_all.reshape(n_lat, S, nq, HEADS, HEAD)
    slot = (lat_at * rows + lax.iota(jnp.int32, rows)) // VIS
    live = jnp.concatenate(
        [slot[None, :] < count[:, None], jnp.ones((S, nq), dtype=bool)], 1
    )
    score = jnp.einsum("zsqhd,skhd->shzqk", heads_q, keys, preferred_element_type=F32)
    score = jnp.where(live[:, None, None, None, :], score, -1e30)
    top = jnp.max(score, -1)
    p = jnp.exp(score - top[..., None])
    total = jnp.sum(p, -1)
    part = jnp.einsum("shzqk,skhd->zsqhd", p.astype(B16), values, preferred_element_type=F32)
    scale = jnp.transpose(1.0 / total, (2, 0, 3, 1))[..., None]
    part = (part * scale).astype(B16).reshape(n_lat, S * nq, inner)
    stats = jnp.stack([top, total], 0).reshape(2 * S * HEADS, n_lat * nq)
    part_all, stats_all = ex("lat", [part, stats], ["swap", "gather"])
    stats_all = stats_all.reshape(n_lat, 2, S, HEADS, n_lat, nq)
    tops, totals = stats_all[:, 0], stats_all[:, 1]
    top_max = jnp.max(tops, 0)
    weight = totals * jnp.exp(tops - top_max)
    whole = jnp.sum(weight, 0)
    lse = top_max + jnp.log(whole)
    weight = lax.dynamic_index_in_dim(weight / whole, lat_at, 3, keepdims=False)
    weight = jnp.transpose(weight, (0, 1, 3, 2)).reshape(n_lat, S * nq, HEADS, 1)
    attended_f = jnp.sum(part_all.reshape(n_lat, S * nq, HEADS, HEAD).astype(F32) * weight, 0)
    attended = attended_f.reshape(S * nq, inner).astype(B16)

    hidden = lat + mm(attended, wo_all)
    ffn_unit, ffn_factor = norm_parts(hidden)
    ff_norm = (ffn_unit * params[4] + params[5]).astype(B16)
    (ffn_all,) = ex("dp", [ff_norm], ["gather"])
    ffn_all = ffn_all.reshape(-1, width)
    up = mm(ffn_all, wup_s)
    act_f, pull = jax.vjp(lambda v: jax.nn.gelu(v, approximate=False), up)
    act = act_f.astype(B16)
    d_act = mm_nt(cot_all, wdown)
    d_up = pull(d_act)[0].astype(B16)
    out_part = mm(act, wdown).astype(B16).reshape(n_dp, S * nq, width)
    d_ffn_part = mm_nt(d_up, wup_s).astype(B16).reshape(n_dp, S * nq, width)
    d_ffn_all, out_all = ex("dp", [d_ffn_part, out_part], ["swap", "swap"])
    latents_out = (hidden + jnp.sum(out_all.astype(F32), 0)).astype(B16)
    d_ffn = jnp.sum(d_ffn_all.astype(F32), 0)
    grad_down = mm_tn(act, cot_all)
    grad_up = mm_tn(ffn_all, d_up)
    d_h, grad_gf, grad_bf = norm_back(d_ffn, ffn_unit, ffn_factor, params[4])
    d_hidden = cot.astype(F32) + d_h
    d_attn = d_hidden.astype(B16)
    grad_out = mm_tn(attended, d_attn)
    d_att = mm_nt(d_attn, wo_all).astype(B16)
    delta = jnp.sum(
        (d_att.astype(F32) * attended_f.reshape(S * nq, inner)).reshape(S * nq, HEADS, HEAD), -1
    )
    d_att_all, delta_all = ex("lat", [d_att, delta.T], ["gather", "gather"])
    d_att_h = d_att_all.reshape(n_lat, S, nq, HEADS, HEAD)
    delta_h = jnp.transpose(delta_all.reshape(n_lat, HEADS, S, nq), (2, 1, 0, 3))[..., None]
    prob = jnp.exp(score - lse[..., None])
    d_prob = jnp.einsum("zsqhd,skhd->shzqk", d_att_h, values, preferred_element_type=F32)
    d_score = (prob * (d_prob - delta_h)).astype(B16)
    dq_part = jnp.einsum("shzqk,skhd->zsqhd", d_score, keys, preferred_element_type=F32)
    (dq_all,) = ex("lat", [dq_part.astype(B16).reshape(n_lat, S * nq, inner)], ["swap"])
    d_keys = jnp.einsum("shzqk,zsqhd->skhd", d_score, heads_q, preferred_element_type=F32)
    d_values = jnp.einsum(
        "shzqk,zsqhd->skhd", prob.astype(B16), d_att_h, preferred_element_type=F32
    )
    d_kv = jnp.concatenate(
        [d_keys.reshape(S, kc, inner), d_values.reshape(S, kc, inner)], -1
    ).astype(B16)
    d_kv_med = d_kv[:, :rows].reshape(S * rows, 2 * inner)
    d_kv_lat = d_kv[:, rows:].reshape(S * nq, 2 * inner)
    grad_kv = mm_tn(med_norm, d_kv_med) + mm_tn(lat_norm, d_kv_lat)
    d_mnorm = mm_nt(d_kv_med, wkv_all)
    d_media, grad_gm, grad_bm = norm_back(d_mnorm, med_unit, med_factor, params[0])
    dq = (jnp.sum(dq_all.astype(F32), 0) * 0.125).astype(B16)
    grad_q = mm_tn(lat_norm, dq)
    d_lnorm = mm_nt(dq, wq_all) + mm_nt(d_kv_lat, wkv_all)
    d_latn, grad_gl, grad_bl = norm_back(d_lnorm, lat_unit, lat_factor, params[2])
    latent_grad = (d_hidden + d_latn).astype(B16)

    smalls = jnp.stack([grad_gm, grad_bm, grad_gl, grad_bl, grad_gf, grad_bf], 0)
    smalls = jnp.transpose(smalls.reshape(6, n_dp, d_part), (1, 0, 2))
    small_s, q_s, kv_s, o_s, up_s = ex(
        "dp",
        [
            smalls,
            grad_q.astype(B16).reshape(n_dp, d_part, inner),
            grad_kv.astype(B16).reshape(n_dp, d_part, 2 * inner),
            grad_out.astype(B16).reshape(n_dp, inner // n_dp, width),
            grad_up.astype(B16).reshape(n_dp, d_part, ff_part),
        ],
        ["swap"] * 5,
    )
    small_s = jnp.sum(small_s, 0)
    q_s = jnp.sum(q_s.astype(F32), 0)
    kv_s = jnp.sum(kv_s.astype(F32), 0)
    o_s = jnp.sum(o_s.astype(F32), 0)
    up_s = jnp.transpose(up_s, (1, 0, 2)).reshape(d_part, ff)
    pieces = [q_s, kv_s, o_s, up_s, grad_down]
    cut = [x.astype(B16).reshape(n_lat, x.shape[0] // n_lat, x.shape[1]) for x in pieces]
    got = ex("lat", cut + [small_s], ["swap"] * 5 + ["gather"])
    small_s = jnp.sum(got[5], 0)
    summed = [jnp.sum(x.astype(F32), 0).astype(B16) for x in got[:5]]
    full = ex("lat", summed, ["gather"] * 5)
    grads = [x.reshape(y.shape).astype(F32) for x, y in zip(full, pieces)]
    return (
        latents_out.reshape(latents.shape),
        d_media.astype(B16).reshape(media.shape),
        latent_grad.reshape(latents.shape),
        *[small_s[i] for i in range(6)],
        *grads,
    )


def solution(mesh):
    rows4 = P(None, "dp", "lat", None)
    vec = P("dp")
    mat = P("dp", None)
    return jax.shard_map(
        functools.partial(shards, mesh.shape["dp"], mesh.shape["lat"]),
        mesh=mesh,
        in_specs=(rows4, rows4, P(None, "dp"), rows4) + (vec,) * 6 + (mat,) * 5,
        out_specs=(rows4,) * 3 + (vec,) * 6 + (mat,) * 5,
        check_vma=False,
    )
```

time: 3260 us -> 610 us (0.19)
  the two profiles are of different devices: /device:TPU:0 before, /device:TPU:13 now
where the time goes in v1:
time: 610 us; the launch traced here: 606 us
  Pallas kernels  410 us (67%)
  matrix products  74.8 us (12%)
  other arithmetic  68.4 us (11%)
  local copies, waits for them, and re-layouts  50.8 us (8%)
    pallas_call x11, Pallas kernels, __call__(): pl.pallas_call(functools.partial(exchange_kernel, axis, n, modes), out_sh...  410 us
    dot_general x6, matrix products, mm(): lax.dot_general(a, b, (((1,), (0,)), ((), ())), preferred_element_type=F32)  21.1 us
    dot_general x6, matrix products, mm_nt(): lax.dot_general(a, b, (((1,), (1,)), ((), ())), preferred_element_type=F32)  17.1 us
    dot_general x6, matrix products, mm_tn(): lax.dot_general(a, b, (((0,), (0,)), ((), ())), preferred_element_type=F32)  15.3 us

profile of v1, /device:TPU:13, one launch (start us, length us, event | category | flops | bytes accessed | tf_op | source)
XLA Modules:
  0.0 606.1 jit_solution(13859593610884800800)
XLA Ops:
  6.5 3.3 convert_reduce_fusion
  10.5 4.0 multiply_reduce_fusion.2
  17.5 38.3 %exchange_2.1 = (bf16[8,128,1024]{2,1,0:T(8,128)(2,1)}, bf16[8,128,512]{2,1,0:T(8,128)(2,1)}) custom-call(bf16[128,1024]{1,0:T(8,128)(2,1)} %bitcast.257, bf16[8,128,512]{2,1,0:T(8,128)(2,1)} %bitcast.233), custom_call_target="tpu_custom_call" | custom-call | tf_op jit(solution)/shard_map/exchange_2/pallas_call | solution.py:69
  55.8 49.5 %exchange_1.1 = (bf16[8,6,128]{2,1,0:T(8,128)(2,1)}, bf16[8,128,512]{2,1,0:T(8,128)(2,1)}, bf16[8,128,1024]{2,1,0:T(8,128)(2,1)}, bf16[8,64,1024]{2,1,0:T(8,128)(2,1)}) custom-call(bf16[6,128]{1,0:T(8,128)(2,1)} %stack.57.refs_0_, bf16[128,512]{1,0:T(8,128)(2,1)} %refs_1_.1, bf16[128,1024]{1,0:T(8,128)(2,1)} %refs_2_.1, bf16[64,1024]{1,0:T(8,128)(2,1)} %refs_3_.1), custom_call_target="tpu_custom_call" | custom-call | tf_op jit(solution)/shard_map/exchange_1/pallas_call | solution.py:69
  106.9 2.3 fusion.29.refs_0_
  109.2 2.0 convolution_convert_fusion.8
  111.2 14.6 %exchange_3.1 = bf16[4,128,512]{2,1,0:T(8,128)(2,1)} custom-call(bf16[128,512]{1,0:T(8,128)(2,1)} %fusion.29.refs_0_), custom_call_target="tpu_custom_call" | custom-call | tf_op jit(solution)/shard_map/exchange_3/pallas_call | solution.py:69
  125.8 1.6 reshape.441
  127.5 4.8 add_convert_fusion
  132.4 5.8 convolution_convert_fusion
  138.2 2.8 pad_maximum_fusion
  141.0 4.7 copy.63
  145.7 4.6 copy.61
  150.2 3.0 select_reduce_fusion
  153.2 1.9 fusion.1
  156.8 6.0 fusion.19
  165.4 20.6 %exchange_4.1 = (bf16[4,128,512]{2,1,0:T(8,128)(2,1)}, f32[4,128,64]{2,1,0:T(8,128)}) custom-call(bf16[4,128,512]{2,1,0:T(8,128)(2,1)} %reshape.443.refs_0_, f32[128,64]{1,0:T(8,128)} %reshape.444.refs_1_), custom_call_target="tpu_custom_call" | custom-call | tf_op jit(solution)/shard_map/exchange_4/pallas_call | solution.py:69
  195.1 26.9 %exchange_5.1 = bf16[8,128,1024]{2,1,0:T(8,128)(2,1)} custom-call(bf16[128,1024]{1,0:T(8,128)(2,1)} %add_convert_fusion.6.refs_0_), custom_call_target="tpu_custom_call" | custom-call | tf_op jit(solution)/shard_map/exchange_5/pallas_call | solution.py:69
  222.0 7.9 %multiply_convert_fusion.2 = (bf16[1024,512]{1,0:T(8,128)(2,1)S(1)}, f32[1024,512]{1,0:T(8,128)S(1)}, f32[1024,512]{1,0:T(8,128)S(1)}) fusion(bf16[1024,1024]{1,0:T(8,128)(2,1)} %bitcast.247, bf16[1024,512]{1,0:T(8,128)(2,1)} %bitcast.298), kind=kOutput, calls=%fused_computation.42 | convolution fusion | flops 1107820544 | bytes 8388608 | tf_op jit(solution)/shard_map/dot_general | solution.py:95
  230.0 1.9 add_convert_fusion.2
  231.9 2.3 convolution_convert_fusion.5
  234.1 2.3 convolution_convert_fusion.6
  236.4 2.6 convolution_convert_fusion.2
  239.0 2.6 convolution_convert_fusion.1
  241.6 48.1 %exchange_6.1 = (bf16[8,128,1024]{2,1,0:T(8,128)(2,1)}, bf16[8,128,1024]{2,1,0:T(8,128)(2,1)}) custom-call(bf16[8,128,1024]{2,1,0:T(8,128)(2,1)} %bitcast.251, bf16[8,128,1024]{2,1,0:T(8,128)(2,1)} %bitcast.252), custom_call_target="tpu_custom_call" | custom-call | tf_op jit(solution)/shard_map/exchange_6/pallas_call | solution.py:69
  289.8 4.0 convert_reduce_fusion.1
  297.3 15.6 %exchange_7.1 = (bf16[4,128,512]{2,1,0:T(8,128)(2,1)}, f32[4,8,128]{2,1,0:T(8,128)}) custom-call(bf16[128,512]{1,0:T(8,128)(2,1)} %get-tuple-element.110.refs_0_, f32[8,128]{1,0:T(8,128)} %bitcast.288), custom_call_target="tpu_custom_call" | custom-call | tf_op jit(solution)/shard_map/exchange_7/pallas_call | solution.py:69
  314.0 2.4 reshape.456
  316.4 5.2 multiply_convert_fusion.1
  321.9 3.2 bitcast_convert_fusion
  326.4 2.7 bitcast_convert_fusion.1
  329.1 4.6 copy.77
  336.4 15.0 %exchange_8.1 = bf16[4,128,512]{2,1,0:T(8,128)(2,1)} custom-call(bf16[4,128,512]{2,1,0:T(8,128)(2,1)} %reshape.462.refs_0_), custom_call_target="tpu_custom_call" | custom-call | tf_op jit(solution)/shard_map/exchange_8/pallas_call | solution.py:69
  352.5 4.6 copy.78
  361.5 5.9 fusion.53
  367.4 2.1 add_convert_fusion.1
  375.2 10.0 %multiply_reduce_fusion = (f32[1024]{0:T(1024)S(1)}, f32[2560]{0:T(1024)S(1)}, f32[2560]{0:T(1024)S(1)}, f32[1024]{0:T(1024)S(1)}, f32[2560,1024]{1,0:T(8,128)}) fusion(bf16[4,2,320,1024]{3,2,1,0:T(8,128)(2,1)S(1)} %bitcast.210, f32[2560]{0:T(1024)S(1)} %copy-done.29, f32[2560]{0:T(1024)S(1)} %copy-done.30, f32[1024]{0:T(1024)S(1)} %bitcast.279, ...), kind=kOutput, calls=%fused_computation.2 | convolution fusion | flops 5394916352 | bytes 23121920 | tf_op jit(solution)/shard_map/dot_general | solution.py:99
  385.9 60.5 %exchange_9.1 = (f32[8,6,128]{2,1,0:T(8,128)}, bf16[8,128,512]{2,1,0:T(8,128)(2,1)}, bf16[8,128,1024]{2,1,0:T(8,128)(2,1)}, bf16[8,64,1024]{2,1,0:T(8,128)(2,1)}, bf16[8,128,512]{2,1,0:T(8,128)(2,1)}) custom-call(f32[8,6,128]{2,1,0:T(8,128)} %bitcast.271, bf16[8,128,512]{2,1,0:T(8,128)(2,1)} %bitcast.231, bf16[8,128,1024]{2,1,0:T(8,128)(2,1)} %bitcast.222, ...), custom_call_target="tpu_custom_call" | custom-call | tf_op jit(solution)/shard_map/exchange_9/pallas_call | solution.py:69
  446.4 2.1 reduce_sum.364
  449.9 9.6 %multiply_convert_fusion = bf16[2560,1024]{1,0:T(8,128)(2,1)} fusion(bf16[4,2,320,1024]{3,2,1,0:T(8,128)(2,1)} %param.15, f32[2560,1024]{1,0:T(8,128)} %get-tuple-element.111, f32[2560]{0:T(1024)S(1)} %broadcast_multiply_fusion, f32[2560]{0:T(1024)S(1)} %copy-done.29, f32[2560]{0:T(1024)S(1)} %broadcast_multiply_fusion.1, f32[1024]{0:T(1024)S(1)} %bitcast.280, ...), kind=kLoop, calls=%fused_computation.3 | loop fusion | flops 23592960 | bytes 21016576 | tf_op jit(solution)/shard_map/convert_element_type | solution.py:250
  461.5 1.8 copy.80
  464.6 60.8 %exchange_10.1 = (bf16[4,32,512]{2,1,0:T(8,128)(2,1)}, bf16[4,32,1024]{2,1,0:T(8,128)(2,1)}, bf16[4,16,1024]{2,1,0:T(8,128)(2,1)}, bf16[4,32,4096]{2,1,0:T(8,128...) custom-call(bf16[4,32,512]{2,1,0:T(8,128)(2,1)} %bitcast.264, bf16[4,32,1024]{2,1,0:T(8,128)(2,1)} %bitcast.258, ...), custom_call_target="tpu_custom_call" | custom-call | tf_op jit(solution)/shard_map/exchange_10/pallas_call | solution.py:69
  531.4 2.2 reduce_sum.372.refs_3_
  533.6 2.2 reduce_sum.373.refs_4_
  535.7 60.4 %exchange_11.1 = (bf16[4,32,512]{2,1,0:T(8,128)(2,1)}, bf16[4,32,1024]{2,1,0:T(8,128)(2,1)}, bf16[4,16,1024]{2,1,0:T(8,128)(2,1)}, bf16[4,32,4096]{2,1,0:T(8,128)(2,1)}, bf16[4,128,1024]{2,1,0:T(8,128)(2,1)}) custom-call(bf16[32,512]{1,0:T(8,128)(2,1)} %reduce_sum.369.refs_0_, bf16[32,1024]{1,0:T(8,128)(2,1)} %reduce_sum.370.refs_1_, ...), custom_call_target="tpu_custom_call" | custom-call | tf_op jit(solution)/shard_map/exchange_11/pallas_call | solution.py:69
  596.2 1.7 bitcast_convert_fusion.6
  599.6 1.9 bitcast_convert_fusion.4
  601.4 2.8 bitcast_convert_fusion.3
  (185 shorter events, 58.9 us)
Async XLA Ops:
  0.6 229.3 %copy-start = (bf16[512,1024]{1,0:T(8,128)(2,1)S(1)}, bf16[512,1024]{1,0:T(8,128)(2,1)}, u32[]{:S(2)}) copy-start(bf16[512,1024]{1,0:T(8,128)(2,1)} %param.29) | copy-start | bytes 3145732
  9.8 5.5 copy-start.26
  15.2 91.4 %copy-start.8 = (bf16[4,2,16,1024]{3,2,1,0:T(8,128)(2,1)S(1)}, bf16[4,2,16,1024]{3,2,1,0:T(8,128)(2,1)}, u32[]{:S(2)}) copy-start(bf16[4,2,16,1024]{3,2,1,0:T(8,128)(2,1)} %param.16) | copy-start | bytes 786436
  106.6 20.9 %copy-start.32 = (f32[1,8,128]{2,0,1:T(1,128)}, f32[1,8,128]{2,0,1:T(1,128)S(1)}, u32[]{:S(2)}) copy-start(f32[1,8,128]{2,0,1:T(1,128)S(1)} %get-tuple-element.97) | copy-start | bytes 12292
  106.9 2.3 copy-start.17
  127.5 22.7 %copy-start.6 = (bf16[4,8,16,8,64]{4,3,2,1,0:T(8,128)(2,1)}, bf16[4,8,16,8,64]{4,3,2,1,0:T(8,128)(2,1)S(1)}, u32[]{:S(2)}) copy-start(bf16[4,8,16,8,64]{4,3,2,1,0:T(8,128)(2,1)S(1)} %reshape.441) | copy-start | bytes 1572868
  127.5 4.9 copy-start.9
  132.4 5.9 copy-start.13
  153.2 2.7 copy-start.2
  188.9 4.7 copy-start.16
  194.0 36.0 %copy-start.38 = (f32[128]{0:T(128)}, f32[128]{0:T(128)S(1)}, u32[]{:S(2)}) copy-start(f32[128]{0:T(128)S(1)} %broadcast_multiply_fusion.8) | copy-start | bytes 1540
  194.2 35.7 %copy-start.40 = (f32[128]{0:T(128)}, f32[128]{0:T(128)S(1)}, u32[]{:S(2)}) copy-start(f32[128]{0:T(128)S(1)} %add_rsqrt_fusion.2) | copy-start | bytes 1540
  222.0 7.9 %copy-start.23 = (bf16[8,128,1024]{2,1,0:T(8,128)(2,1)S(1)}, bf16[8,128,1024]{2,1,0:T(8,128)(2,1)}, u32[]{:S(2)}) copy-start(bf16[8,128,1024]{2,1,0:T(8,128)(2,1)} %get-tuple-element.49) | copy-start | bytes 6291460
  231.9 2.3 copy-start.22
  234.1 2.3 copy-start.44
  289.7 4.0 copy-start.39
  289.7 4.0 copy-start.41
  289.7 4.8 copy-start.25
  293.8 1.7 copy-start.20
  295.4 26.2 %copy-start.11 = (f32[128,1024]{1,0:T(8,128)}, f32[128,1024]{1,0:T(8,128)S(1)}, u32[]{:S(2)}) copy-start(f32[128,1024]{1,0:T(8,128)S(1)} %get-tuple-element.89) | copy-start | bytes 1572868
  295.4 21.0 %copy-start.28 = (f32[8,4,8,16]{3,2,1,0:T(8,128)S(1)}, f32[8,4,8,16]{3,2,1,0:T(8,128)}, u32[]{:S(2)}) copy-start(f32[8,4,8,16]{3,2,1,0:T(8,128)} %log_add_fusion) | copy-start | bytes 49156
  313.0 8.7 %slice-start.2 = ((s8[6291456]{0:T(1024)(128)(4,1)}), s8[2097152]{0:T(1024)(128)(4,1)S(1)}, s32[]{:S(2)}) async-start(s8[6291456]{0:T(1024)(128)(4,1)} %bitcast.211), calls=%async_computation.2 | async-start | bytes 4194304
  316.4 5.2 slice-start.3
  316.4 5.5 copy-start.14
  321.9 3.2 copy-start.3
  325.1 1.3 copy-start.7
  357.1 1.9 copy-start.4
  357.1 2.7 copy-start.5
  357.1 4.0 slice-start.4
  359.8 1.7 slice-start.5
  361.5 5.9 copy-start.18
  367.4 2.1 copy-start.10
  369.4 1.2 copy-start.42
  369.4 1.2 copy-start.43
  369.4 1.9 copy-start.12
  369.5 5.7 slice-start
  370.7 4.5 slice-start.1
  371.3 3.9 copy-start.29
  371.3 3.9 copy-start.30
  371.3 3.9 copy-start.33
  375.2 10.0 %copy-start.35 = (f32[1024]{0:T(1024)S(1)}, f32[1024]{0:T(1024)}, u32[]{:S(2)}) copy-start(f32[1024]{0:T(1024)} %get-tuple-element.76) | copy-start | bytes 12292
  375.2 10.0 %copy-start.37 = (f32[1024]{0:T(1024)S(1)}, f32[1024]{0:T(1024)}, u32[]{:S(2)}) copy-start(f32[1024]{0:T(1024)} %get-tuple-element.74) | copy-start | bytes 12292
  385.9 63.9 %copy-start.31 = (f32[2560]{0:T(1024)S(1)}, f32[2560]{0:T(1024)}, u32[]{:S(2)}) copy-start(f32[2560]{0:T(1024)} %rsqrt.35) | copy-start | bytes 30724
  385.9 63.9 %copy-start.34 = (f32[1,8,128]{2,0,1:T(1,128)S(1)}, f32[1,8,128]{2,0,1:T(1,128)}, u32[]{:S(2)}) copy-start(f32[1,8,128]{2,0,1:T(1,128)} %copy-done.32) | copy-start | bytes 12292
  449.9 9.7 %copy-start.27 = (bf16[8,64,1024]{2,1,0:T(8,128)(2,1)S(1)}, bf16[8,64,1024]{2,1,0:T(8,128)(2,1)}, u32[]{:S(2)}) copy-start(bf16[8,64,1024]{2,1,0:T(8,128)(2,1)} %get-tuple-element.56) | copy-start | bytes 3145732
  449.9 10.5 %copy-start.21 = (bf16[8,128,1024]{2,1,0:T(8,128)(2,1)S(1)}, bf16[8,128,1024]{2,1,0:T(8,128)(2,1)}, u32[]{:S(2)}) copy-start(bf16[8,128,1024]{2,1,0:T(8,128)(2,1)} %get-tuple-element.55) | copy-start | bytes 6291460
  596.2 8.0 %copy-start.24 = (bf16[4,128,1024]{2,1,0:T(8,128)(2,1)S(1)}, bf16[4,128,1024]{2,1,0:T(8,128)(2,1)}, u32[]{:S(2)}) copy-start(bf16[4,128,1024]{2,1,0:T(8,128)(2,1)} %get-tuple-element.69) | copy-start | bytes 3145732
  599.6 6.3 %copy-start.1 = (bf16[512,1024]{1,0:T(8,128)(2,1)S(1)}, bf16[512,1024]{1,0:T(8,128)(2,1)}, u32[]{:S(2)}) copy-start(bf16[512,1024]{1,0:T(8,128)(2,1)} %param.29) | copy-start | bytes 3145732
  (3 other events, 2.7 us)

commit v2 on v1

--- a/solution.py
+++ b/solution.py
@@ -1,4 +1,5 @@
 import functools
+import types
 
 import jax
 import jax.numpy as jnp
@@ -15,6 +16,7 @@
 B16 = jnp.bfloat16
 MESH = pl.DeviceIdType.MESH
 DMA = pltpu.SemaphoreType.DMA
+VMEM_BYTES = 62 << 20
 
 
 def exchange_kernel(axis, n, modes, *refs):
@@ -254,12 +256,715 @@
     )
 
 
+NT, NN, TN = (((1,), (1,)), ((), ())), (((1,), (0,)), ((), ())), (((0,), (0,)), ((), ()))
+
+
+def dot(a, b, form):
+    return lax.dot_general(a, b, form, preferred_element_type=F32)
+
+
+def centred(x):
+    mean = jnp.mean(x, -1, keepdims=True)
+    cent = x - mean
+    factor = lax.rsqrt(jnp.mean(cent * cent, -1, keepdims=True) + EPS)
+    return cent * factor, factor
+
+
+def back(grad, unit, factor, gain):
+    scaled = grad * gain
+    inner = jnp.mean(scaled * unit, -1, keepdims=True)
+    return factor * (scaled - jnp.mean(scaled, -1, keepdims=True) - unit * inner)
+
+
+def fused_kernel(geo, refs):
+    S, R, Q, D, I, NC, NZ = geo
+    KR = R + Q
+    B = S * Q
+    G = 2
+    W = I // G
+    HG = HEADS // G
+    r = refs
+    me = lax.axis_index("dp")
+    z = lax.axis_index("lat")
+    chip = me // 2
+    core = lax.rem(me, 2)
+    sib = me + 1 - 2 * core
+    other = 1 - core
+
+    def chip_to(k):
+        return lax.rem(chip + k, NC)
+
+    def chip_from(k):
+        return lax.rem(chip + NC - k, NC)
+
+    def z_to(k):
+        return lax.rem(z + k, NZ)
+
+    def z_from(k):
+        return lax.rem(z + NZ - k, NZ)
+
+    quads = range(1, NC)
+    planes = range(1, NZ)
+    used = [0, 0]
+
+    def local(src, dst):
+        sem = r.lsem.at[used[0]]
+        used[0] += 1
+        copy = pltpu.make_async_copy(src, dst, sem)
+        copy.start()
+        return copy
+
+    def remote(src, dst, **where):
+        at = used[1]
+        used[1] += 1
+        copy = pltpu.make_async_remote_copy(
+            src, dst, r.ssem.at[at], r.rsem.at[at], device_id=where, device_id_type=MESH
+        )
+        copy.start()
+        return copy
+
+    class Spread:
+        def __init__(self, src_for, dst):
+            self.dst = dst
+            self.far = [remote(src_for(chip_to(k)), dst.at[me], dp=2 * chip_to(k) + core) for k in quads]
+            self.near = remote(src_for(chip), dst.at[me], dp=sib)
+            self.own = local(src_for(chip), dst.at[me])
+
+        def forward(self):
+            self.passed = []
+            for k in quads:
+                self.far[k - 1].wait_recv()
+                slot = self.dst.at[2 * chip_from(k) + core]
+                self.passed.append(remote(slot, slot, dp=sib))
+
+        def finish(self):
+            self.own.wait()
+            self.near.wait()
+            for copy in self.far:
+                copy.wait_send()
+            for copy in self.passed:
+                copy.wait()
+
+    def to_quad(src_for, dst):
+        return [remote(src_for(chip_to(k)), dst, dp=2 * chip_to(k) + core) for k in quads]
+
+    def to_planes(src_for, dst):
+        return [remote(src_for(z_to(k)), dst, lat=z_to(k)) for k in planes]
+
+    def wait_all(copies):
+        for copy in copies:
+            copy.wait()
+
+    barrier = pltpu.get_barrier_semaphore()
+    for k in quads:
+        pl.semaphore_signal(barrier, inc=1, device_id={"dp": 2 * chip_to(k) + core}, device_id_type=MESH)
+    pl.semaphore_signal(barrier, inc=1, device_id={"dp": sib}, device_id_type=MESH)
+    for k in planes:
+        pl.semaphore_signal(barrier, inc=1, device_id={"lat": z_to(k)}, device_id_type=MESH)
+    pl.semaphore_wait(barrier, NC - 1 + 1 + NZ - 1)
+
+    g_small = Spread(lambda _: r.small, r.small_all)
+    g_wq = Spread(lambda _: r.wq, r.wq_all)
+    lat_in = local(r.lat, r.lat_v)
+    cot_in = local(r.cot, r.cot4.at[chip])
+    slots = r.med.shape[0]
+
+    def med_copy(s):
+        slot = lax.rem(s, slots)
+        return pltpu.make_async_copy(r.media.at[s], r.med.at[slot], r.dsem.at[slot])
+
+    def med_first():
+        for s in range(slots):
+            med_copy(jnp.int32(s)).start()
+
+    def med_next(s):
+        @pl.when(s + slots < S)
+        def _():
+            med_copy(s + slots).start()
+
+    med_first()
+    g_wkv = Spread(lambda _: r.wkv, r.wkv_all)
+    g_wo = Spread(lambda _: r.wo, r.wo_all)
+    g_small.forward()
+    g_small.finish()
+    params = r.params
+    for d in range(2 * NC):
+        span = D // (2 * NC)
+        params[:, d * span : (d + 1) * span] = r.small_all[d]
+
+    def param(i):
+        return params[i : i + 1, :]
+
+    lat_in.wait()
+    unit, _ = centred(r.lat_v[...].astype(F32))
+    r.latn[...] = (unit * param(2) + param(3)).astype(B16)
+    g_wq.forward()
+
+    rb = 64
+
+    def norm_sample(s, carry):
+        slot = lax.rem(s, slots)
+        med_copy(s).wait()
+
+        def part(i, inner):
+            x = r.med[slot, pl.ds(pl.multiple_of(i * rb, rb), rb), :].astype(F32)
+            u, _ = centred(x)
+            row = pl.multiple_of(s * KR + i * rb, 16)
+            r.X[pl.ds(row, rb), :] = (u * param(0) + param(1)).astype(B16)
+            return inner
+
+        lax.fori_loop(0, R // rb, part, 0)
+        row = pl.multiple_of(s * KR + R, 16)
+        at = pl.multiple_of(s * Q, 16)
+        r.X[pl.ds(row, Q), :] = r.latn[pl.ds(at, Q), :]
+        med_next(s)
+        return carry
+
+    g_wq.finish()
+    query = dot(r.latn[...], r.wq_all[...].reshape(D, I), NN) * 0.125
+    r.q_all[z] = query.astype(B16).reshape(S, Q, I)
+    q_out = to_planes(lambda _: r.q_all.at[z], r.q_all.at[z])
+    lax.fori_loop(0, S, norm_sample, 0)
+    med_first()
+    g_wkv.forward()
+    g_wo.forward()
+    g_wkv.finish()
+    span = r.wup_all.shape[2]
+
+    def up_slice(k):
+        return r.wup.at[:, pl.ds(pl.multiple_of(k * span, 128), span)]
+
+    cot_in.wait()
+    g_cot = to_quad(lambda _: r.cot, r.cot4.at[chip])
+    g_down = remote(r.wdown, r.wdown2.at[core], dp=sib)
+    g_down_own = local(r.wdown, r.wdown2.at[core])
+    g_up = Spread(up_slice, r.wup_all)
+
+    def keyval(s, carry):
+        rows = pl.ds(pl.multiple_of(s * KR, 16), KR)
+        r.KV[rows, :] = dot(r.X[rows, :], r.wkv_all[...].reshape(D, 2 * I), NN).astype(B16)
+        return carry
+
+    lax.fori_loop(0, S, keyval, 0)
+    g_wo.finish()
+    wait_all(q_out)
+
+    own_head = (
+        lax.broadcasted_iota(jnp.int32, (HG * NZ * Q, W), 0) // (NZ * Q)
+        == lax.broadcasted_iota(jnp.int32, (HG * NZ * Q, W), 1) // HEAD
+    )
+    r.mask[...] = own_head.astype(F32).astype(B16)
+
+    def spread_heads(x):
+        return jnp.concatenate([x] * HG, 0) * r.mask[...]
+
+    def take_heads(x):
+        low = lax.broadcasted_iota(jnp.int32, (NZ * Q, 2 * HEAD), 1) < HEAD
+        cols = []
+        for pair in range(HG // 2):
+            block = x[:, pair * 2 * HEAD : (pair + 1) * 2 * HEAD]
+            n = NZ * Q
+            cols.append(
+                jnp.where(low, block[2 * pair * n : (2 * pair + 1) * n], block[(2 * pair + 1) * n : (2 * pair + 2) * n])
+            )
+        return jnp.concatenate(cols, 1)
+
+    def scores(s, g, qbig):
+        rows = pl.ds(pl.multiple_of(s * KR, 16), KR)
+        raw = dot(r.KV[rows, g * W : (g + 1) * W], qbig, NT)
+        row = lax.broadcasted_iota(jnp.int32, raw.shape, 0)
+        live = jnp.logical_or(row >= R, row + z * R < r.counts[s] * VIS)
+        return jnp.where(live, raw, -1e30)
+
+    def queries(s, g):
+        return spread_heads(r.q_all[:, s, :, g * W : (g + 1) * W].reshape(NZ * Q, W))
+
+    def stats(s, carry):
+        for g in range(G):
+            score = scores(s, g, queries(s, g))
+            top = jnp.max(score, 0, keepdims=True)
+            total = jnp.sum(jnp.exp(score - top), 0, keepdims=True)
+            r.lse[z, pl.ds(s * G + g, 1), :] = top + jnp.log(total)
+        return carry
+
+    lax.fori_loop(0, S, stats, 0)
+    wait_all(to_planes(lambda _: r.lse.at[z], r.lse.at[z]))
+    every = r.lse[...]
+    top = jnp.max(every, 0)
+    r.lse_all[...] = top + jnp.log(jnp.sum(jnp.exp(every - top[None]), 0))
+
+    def attend(s, carry):
+        rows = pl.ds(pl.multiple_of(s * KR, 16), KR)
+        for g in range(G):
+            score = scores(s, g, queries(s, g))
+            prob = jnp.exp(score - r.lse_all[pl.ds(s * G + g, 1), :])
+            part = dot(prob.astype(B16), r.KV[rows, I + g * W : I + (g + 1) * W], TN)
+            r.o_send[:, s, :, g * W : (g + 1) * W] = take_heads(part).astype(B16).reshape(NZ, Q, W)
+        return carry
+
+    lax.fori_loop(0, S, attend, 0)
+    o_out = to_planes(lambda k: r.o_send.at[k], r.o_recv.at[z])
+    g_up.forward()
+    wait_all(g_cot)
+    g_down.wait()
+    g_down_own.wait()
+
+    def act_grad(b, carry):
+        r.d_act[b] = dot(r.cot4[b], r.wdown2[...].reshape(span, D), NT)
+        return carry
+
+    lax.fori_loop(0, NC, act_grad, 0)
+    g_up.finish()
+    wait_all(o_out)
+    att = r.o_send[z].astype(F32)
+    for k in planes:
+        att = att + r.o_recv[z_from(k)].astype(F32)
+    att = att.reshape(B, I)
+    r.att_f[...] = att
+    r.att[...] = att.astype(B16)
+    hidden = r.lat_v[...].astype(F32) + dot(r.att[...], r.wo_all[...].reshape(I, D), NN)
+    r.hidden[...] = hidden
+    unit, _ = centred(hidden)
+    r.ffn4[chip] = (unit * param(4) + param(5)).astype(B16)
+    f_out = to_quad(lambda _: r.ffn4.at[chip], r.ffn4.at[chip])
+
+    def feed(b):
+        r.up[...] = dot(r.ffn4[b], r.wup_all[...].reshape(D, span), NN)
+
+        def gelu_part(i, carry):
+            rows = pl.ds(pl.multiple_of(i * 32, 32), 32)
+            x = r.up[rows, :]
+            cdf = 0.5 * (1.0 + lax.erf(x * 0.7071067811865476))
+            pdf = jnp.exp(-0.5 * x * x) * 0.3989422804014327
+            r.act[b, rows, :] = (x * cdf).astype(B16)
+            r.d_up[b, rows, :] = (r.d_act[b, rows, :] * (cdf + x * pdf)).astype(B16)
+            return carry
+
+        lax.fori_loop(0, B // 32, gelu_part, 0)
+        r.df_send[b] = dot(r.d_up[b], r.wup_all[...].reshape(D, span), NT).astype(B16)
+
+    feed(chip)
+    df_out = []
+    for k in quads:
+        f_out[k - 1].wait_recv()
+        b = chip_from(k)
+        feed(b)
+        df_out.append(remote(r.df_send.at[b], r.df_recv.at[chip], dp=2 * b + core))
+
+    def down(i, carry):
+        r.out_send[i] = dot(r.act[i], r.wdown2[...].reshape(span, D), NN).astype(B16)
+        return carry
+
+    lax.fori_loop(0, NC, down, 0)
+    out_out = to_quad(lambda k: r.out_send.at[k], r.out_recv.at[chip])
+
+    half = span // 2
+    act2 = r.act
+
+    def grad_down(i, carry):
+        at = pl.multiple_of(i * 256, 256)
+        value = dot(
+            act2[:, :, pl.ds(at, 256)].reshape(NC * B, 256), r.cot4[...].reshape(NC * B, D), TN
+        )
+        r.gd[i // (half // 256), pl.ds(pl.multiple_of(lax.rem(i * 256, half), 256), 256), :] = value.astype(B16)
+        return carry
+
+    lax.fori_loop(0, span // 256, grad_down, 0)
+    gd_out = remote(r.gd.at[other], r.gd_recv, dp=sib)
+    dw = D // NC
+    hw = dw // 2
+
+    def grad_up(i, carry):
+        at = pl.multiple_of(i * dw, dw)
+        value = dot(
+            r.ffn4[:, :, pl.ds(at, dw)].reshape(NC * B, dw), r.d_up[...].reshape(NC * B, span), TN
+        ).astype(B16)
+        r.gu[0, i] = value[:hw]
+        r.gu[1, i] = value[hw:]
+        return carry
+
+    lax.fori_loop(0, NC, grad_up, 0)
+    gu_out = remote(r.gu.at[other], r.gu_recv, dp=sib)
+
+    for copy in f_out:
+        copy.wait_send()
+    wait_all(df_out)
+    d_ffn = r.df_send[chip].astype(F32)
+    for k in quads:
+        d_ffn = d_ffn + r.df_recv[chip_to(k)].astype(F32)
+    unit, factor = centred(r.hidden[...])
+    sums = r.sums
+    sums[4:5, :] = jnp.sum(d_ffn * unit, 0, keepdims=True)
+    sums[5:6, :] = jnp.sum(d_ffn, 0, keepdims=True)
+    d_hidden = r.cot4[chip].astype(F32) + back(d_ffn, unit, factor, param(4))
+    r.d_hidden[...] = d_hidden
+    r.d_attn[...] = d_hidden.astype(B16)
+    d_att = dot(r.d_attn[...], r.wo_all[...].reshape(I, D), NT).astype(B16)
+    weighed = d_att.astype(F32) * r.att_f[...]
+    lane = lax.broadcasted_iota(jnp.int32, (B, 128), 1)
+    delta = jnp.zeros((B, 128), F32)
+    low_lane = lax.broadcasted_iota(jnp.int32, (B, 128), 1) < HEAD
+    for h in range(HEADS):
+        block = weighed[:, (h // 2) * 128 : (h // 2) * 128 + 128]
+        keep = low_lane if h % 2 == 0 else jnp.logical_not(low_lane)
+        one = jnp.sum(jnp.where(keep, block, 0.0), -1, keepdims=True)
+        delta = jnp.where(jnp.logical_or(lane == h, lane == HEADS + h), -one, delta)
+    coarse = delta.astype(B16).astype(F32)
+    ext = jnp.where(lane < HEADS, coarse, delta - coarse).astype(B16)
+    r.d_ext[z, :, :, 0:I] = d_att.reshape(S, Q, I)
+    r.d_ext[z, :, :, I : I + 128] = ext.reshape(S, Q, 128)
+    d_out = to_planes(lambda _: r.d_ext.at[z], r.d_ext.at[z])
+
+    ow = I // NC
+    oh = ow // 2
+    for i in range(NC):
+        value = dot(r.att[:, i * ow : (i + 1) * ow], r.d_attn[...], TN).astype(B16)
+        r.go[0, i] = value[:oh]
+        r.go[1, i] = value[oh:]
+    go_out = remote(r.go.at[other], r.go_recv, dp=sib)
+
+    wait_all(out_out)
+    out = r.hidden[...] + r.out_send[chip].astype(F32)
+    for k in quads:
+        out = out + r.out_recv[chip_to(k)].astype(F32)
+    r.stage[0] = out.astype(B16)
+    put_out = local(r.stage.at[0], r.latents_out)
+
+    def add_pair(dst, a, b, n):
+        def body(i, carry):
+            dst[i] = (a[i].astype(F32) + b[i].astype(F32)).astype(B16)
+            return carry
+
+        lax.fori_loop(0, n, body, 0)
+
+    gd_out.wait()
+    piece = half // NZ
+    for j in range(NZ):
+        rows = slice(j * piece, (j + 1) * piece)
+        r.gd_sum[j] = (r.gd[core, rows, :].astype(F32) + r.gd_recv[rows, :].astype(F32)).astype(B16)
+    gz_out = to_planes(lambda k: r.gd_sum.at[k], r.gz_recv.at[0, z])
+    gu_out.wait()
+    add_pair(r.gu_sum, r.gu.at[core], r.gu_recv, NC)
+    gq_out = to_quad(lambda k: r.gu_sum.at[k], r.gu_quad.at[chip])
+    wait_all(d_out)
+
+    ones = jnp.ones((KR, 128), B16)
+    lane_e = lax.broadcasted_iota(jnp.int32, (HG * NZ * Q, 128), 1)
+    head_e = lax.broadcasted_iota(jnp.int32, (HG * NZ * Q, 128), 0) // (NZ * Q)
+    for g in range(G):
+        r.mask_e[g] = (
+            jnp.logical_or(lane_e == head_e + g * HG, lane_e == head_e + g * HG + HEADS).astype(F32).astype(B16)
+        )
+
+    def attend_back(s, carry):
+        rows = pl.ds(pl.multiple_of(s * KR, 16), KR)
+        for g in range(G):
+            qbig = queries(s, g)
+            score = scores(s, g, qbig)
+            prob = jnp.exp(score - r.lse_all[pl.ds(s * G + g, 1), :])
+            dbig = spread_heads(r.d_ext[:, s, :, g * W : (g + 1) * W].reshape(NZ * Q, W))
+            minus = r.d_ext[:, s, :, I : I + 128].reshape(NZ * Q, 128)
+            minus = jnp.concatenate([minus] * HG, 0) * r.mask_e[g]
+            d_prob = dot(r.KV[rows, I + g * W : I + (g + 1) * W], dbig, NT) + dot(ones, minus, NT)
+            d_score = (prob * d_prob).astype(B16)
+            dq = dot(d_score, r.KV[rows, g * W : (g + 1) * W], TN)
+            r.dq_send[:, s, :, g * W : (g + 1) * W] = take_heads(dq).astype(B16).reshape(NZ, Q, W)
+            r.KV[rows, g * W : (g + 1) * W] = dot(d_score, qbig, NN).astype(B16)
+            r.KV[rows, I + g * W : I + (g + 1) * W] = dot(prob.astype(B16), dbig, NN).astype(B16)
+        return carry
+
+    lax.fori_loop(0, S, attend_back, 0)
+    dq_out = to_planes(lambda k: r.dq_send.at[k], r.dq_recv.at[z])
+
+    wait_all(gq_out)
+    r.gu_quad[chip] = r.gu_sum[chip]
+    gz_out += to_planes(lambda k: r.gu_quad.at[k], r.gz_recv.at[1, z])
+
+    def grad_kv(i, carry):
+        at = pl.multiple_of(i * dw, dw)
+        value = dot(r.X[:, pl.ds(at, dw)], r.KV[...], TN).astype(B16)
+        r.gk[0, i] = value[:hw]
+        r.gk[1, i] = value[hw:]
+        return carry
+
+    lax.fori_loop(0, NC, grad_kv, 0)
+    gk_out = remote(r.gk.at[other], r.gk_recv, dp=sib)
+
+    wait_all(dq_out)
+    dq = r.dq_send[z].astype(F32)
+    for k in planes:
+        dq = dq + r.dq_recv[z_from(k)].astype(F32)
+    r.dq[...] = (dq.reshape(B, I) * 0.125).astype(B16)
+    for i in range(NC):
+        value = dot(r.latn[:, i * dw : (i + 1) * dw], r.dq[...], TN).astype(B16)
+        r.gq[0, i] = value[:hw]
+        r.gq[1, i] = value[hw:]
+    gqs_out = remote(r.gq.at[other], r.gq_recv, dp=sib)
+    gk_out.wait()
+    go_out.wait()
+    add_pair(r.gk_sum, r.gk.at[core], r.gk_recv, NC)
+    add_pair(r.go_sum, r.go.at[core], r.go_recv, NC)
+    quad_out = to_quad(lambda k: r.gk_sum.at[k], r.gk_quad.at[chip])
+    quad_out += to_quad(lambda k: r.go_sum.at[k], r.go_quad.at[chip])
+    gqs_out.wait()
+    add_pair(r.gq_sum, r.gq.at[core], r.gq_recv, NC)
+    quad_out += to_quad(lambda k: r.gq_sum.at[k], r.gq_quad.at[chip])
+
+    wait_all(gz_out)
+    for a, own in enumerate([r.gd_sum, r.gu_quad]):
+        total = own[z].astype(F32)
+        for k in planes:
+            total = total + r.gz_recv[a, z_from(k)].astype(F32)
+        r.gz_sum[a] = total.astype(B16)
+    last = []
+    for a, out in enumerate([r.gdown, r.gup]):
+        last.append(local(r.gz_sum.at[a], out.at[z]))
+        last += to_planes(lambda _: r.gz_sum.at[a], out.at[z])
+
+    sums[0:1, :] = jnp.zeros((1, D), F32)
+    sums[1:2, :] = jnp.zeros((1, D), F32)
+    sums[6:8, :] = jnp.zeros((2, D), F32)
+
+    def media_back(s, carry):
+        slot = lax.rem(s, 2)
+        held = lax.rem(s, slots)
+        rows = pl.ds(pl.multiple_of(s * KR, 16), KR)
+        med_copy(s).wait()
+        r.dn[...] = dot(r.KV[rows, :], r.wkv_all[...].reshape(D, 2 * I), NT)
+        r.d_lat[pl.ds(pl.multiple_of(s * Q, 8), Q), :] = r.dn[R:, :]
+
+        @pl.when(s >= 2)
+        def _():
+            pltpu.make_async_copy(r.mg.at[slot], r.media_grad.at[s - 2], r.msem.at[slot]).wait()
+
+        def part(i, inner):
+            block = pl.ds(pl.multiple_of(i * rb, rb), rb)
+            unit, factor = centred(r.med[held, block, :].astype(F32))
+            grad = r.dn[block, :]
+            sums[0:1, :] += jnp.sum(grad * unit, 0, keepdims=True)
+            sums[1:2, :] += jnp.sum(grad, 0, keepdims=True)
+            r.mg[slot, block, :] = back(grad, unit, factor, param(0)).astype(B16)
+            return inner
+
+        lax.fori_loop(0, R // rb, part, 0)
+        pltpu.make_async_copy(r.mg.at[slot], r.media_grad.at[s], r.msem.at[slot]).start()
+        med_next(s)
+        return carry
+
+    lax.fori_loop(0, S, media_back, 0)
+
+    d_latn = r.d_lat[...] + dot(r.dq[...], r.wq_all[...].reshape(D, I), NT)
+    unit, factor = centred(r.lat_v[...].astype(F32))
+    sums[2:3, :] = jnp.sum(d_latn * unit, 0, keepdims=True)
+    sums[3:4, :] = jnp.sum(d_latn, 0, keepdims=True)
+    r.stage[1] = (r.d_hidden[...] + back(d_latn, unit, factor, param(2))).astype(B16)
+    put_lat = local(r.stage.at[1], r.latent_grad)
+
+    sp = D // (2 * NC)
+    for t in range(NC):
+        for cc in range(2):
+            d = 2 * t + cc
+            r.sm[cc, t] = sums[:, d * sp : (d + 1) * sp]
+    sm_out = remote(r.sm.at[other], r.sm_recv, dp=sib)
+    sm_out.wait()
+    r.sm_sum[...] = r.sm[core] + r.sm_recv[...]
+    quad_out += to_quad(lambda k: r.sm_sum.at[k], r.sm_quad.at[chip])
+    wait_all(quad_out)
+
+    def quad_total(own, got):
+        total = own[chip].astype(F32)
+        for k in quads:
+            total = total + got[chip_to(k)].astype(F32)
+        return total
+
+    r.sm_z[z] = quad_total(r.sm_sum, r.sm_quad)
+    zs_out = to_planes(lambda _: r.sm_z.at[z], r.sm_z.at[z])
+    thirds = [
+        (r.gk_sum, r.gk_quad, r.gk_z, r.gk_zr, r.gk_f, r.gkv),
+        (r.gq_sum, r.gq_quad, r.gq_z, r.gq_zr, r.gq_f, r.gquery),
+        (r.go_sum, r.go_quad, r.go_z, r.go_zr, r.go_f, r.gout),
+    ]
+    for own, got, split, far, _, _ in thirds:
+        total = quad_total(own, got).astype(B16)
+        rows = total.shape[0] // NZ
+        for j in range(NZ):
+            split[j] = total[j * rows : (j + 1) * rows]
+        zs_out += to_planes(lambda k: split.at[k], far.at[z])
+    wait_all(zs_out)
+    r.sm_all[...] = jnp.sum(r.sm_z[...], 0)
+    last.append(local(r.sm_all, r.gsmall))
+    for _, _, split, far, whole, out in thirds:
+        total = split[z].astype(F32)
+        for k in planes:
+            total = total + far[z_from(k)].astype(F32)
+        whole[...] = total.astype(B16)
+        last.append(local(whole, out.at[z]))
+        last += to_planes(lambda _: whole, out.at[z])
+    for slot in range(2):
+        pltpu.make_async_copy(
+            r.mg.at[slot], r.media_grad.at[S - 2 + slot], r.msem.at[slot]
+        ).wait()
+    put_out.wait()
+    put_lat.wait()
+    wait_all(last)
+    assert used[1] <= r.rsem.shape[0] and used[0] <= r.lsem.shape[0]
+
+
+def fused(n_dp, n_lat, media, latents, counts, cotangent, g_m, b_m, g_l, b_l, g_f, b_f, wq, wkv, wo, wup, wdown):
+    micro, per, R, D = media.shape
+    Q = latents.shape[2]
+    S = micro * per
+    B = S * Q
+    I = wq.shape[1]
+    NC = n_dp // 2
+    NZ = n_lat
+    KR = R + Q
+    span = wup.shape[1] // NC
+    dp_rows = D // n_dp
+    small = jnp.stack([g_m, b_m, g_l, b_l, g_f, b_f], 0).astype(F32)
+    small = jnp.pad(small, ((0, 2), (0, 0)))
+    hbm = pl.BlockSpec(memory_space=pl.ANY)
+    ins = dict(
+        media=media.reshape(S, R, D),
+        lat=latents.reshape(B, D),
+        cot=cotangent.reshape(B, D),
+        small=small,
+        wq=wq,
+        wkv=wkv,
+        wo=wo,
+        wup=wup,
+        wdown=wdown,
+        counts=counts.reshape(S),
+    )
+    in_specs = [hbm] * 9 + [pl.BlockSpec(memory_space=pltpu.SMEM)]
+    outs = dict(
+        latents_out=((B, D), B16),
+        media_grad=((S, R, D), B16),
+        latent_grad=((B, D), B16),
+        gsmall=((8, dp_rows), F32),
+        gquery=((NZ, dp_rows // NZ, I), B16),
+        gkv=((NZ, dp_rows // NZ, 2 * I), B16),
+        gout=((NZ, I // n_dp // NZ, D), B16),
+        gup=((NC, dp_rows, span), B16),
+        gdown=((NZ, span // 2 // NZ, D), B16),
+    )
+    kv_rows = S * KR
+    o_rows = I // n_dp
+    buffers = dict(
+        med=((4, R, D), B16),
+        X=((kv_rows, D), B16),
+        KV=((kv_rows, 2 * I), B16),
+        small_all=((n_dp, 8, dp_rows), F32),
+        params=((8, D), F32),
+        wq_all=((n_dp, dp_rows, I), B16),
+        wkv_all=((n_dp, dp_rows, 2 * I), B16),
+        wo_all=((n_dp, o_rows, D), B16),
+        wup_all=((n_dp, dp_rows, span), B16),
+        wdown2=((2, span // 2, D), B16),
+        lat_v=((B, D), B16),
+        latn=((B, D), B16),
+        cot4=((NC, B, D), B16),
+        q_all=((NZ, S, Q, I), B16),
+        lse=((NZ, 2 * S, NZ * Q * HEADS // 2), F32),
+        lse_all=((2 * S, NZ * Q * HEADS // 2), F32),
+        mask=((NZ * Q * HEADS // 2, I // 2), B16),
+        mask_e=((2, NZ * Q * HEADS // 2, 128), B16),
+        o_send=((NZ, S, Q, I), B16),
+        o_recv=((NZ, S, Q, I), B16),
+        att_f=((B, I), F32),
+        att=((B, I), B16),
+        hidden=((B, D), F32),
+        ffn4=((NC, B, D), B16),
+        d_act=((NC, B, span), F32),
+        up=((B, span), F32),
+        act=((NC, B, span), B16),
+        d_up=((NC, B, span), B16),
+        df_send=((NC, B, D), B16),
+        df_recv=((NC, B, D), B16),
+        out_send=((NC, B, D), B16),
+        out_recv=((NC, B, D), B16),
+        gd=((2, span // 2, D), B16),
+        gd_recv=((span // 2, D), B16),
+        gd_sum=((NZ, span // 2 // NZ, D), B16),
+        gu=((2, NC, dp_rows, span), B16),
+        gu_recv=((NC, dp_rows, span), B16),
+        gu_sum=((NC, dp_rows, span), B16),
+        gu_quad=((NC, dp_rows, span), B16),
+        gz_recv=((2, NZ, dp_rows, span), B16),
+        gz_sum=((2, dp_rows, span), B16),
+        d_hidden=((B, D), F32),
+        d_attn=((B, D), B16),
+        d_ext=((NZ, S, Q, I + 128), B16),
+        dq_send=((NZ, S, Q, I), B16),
+        dq_recv=((NZ, S, Q, I), B16),
+        dq=((B, I), B16),
+        d_lat=((B, D), F32),
+        dn=((KR, D), F32),
+        mg=((2, R, D), B16),
+        stage=((2, B, D), B16),
+        sums=((8, D), F32),
+        sm=((2, NC, 8, dp_rows), F32),
+        sm_recv=((NC, 8, dp_rows), F32),
+        sm_sum=((NC, 8, dp_rows), F32),
+        sm_quad=((NC, 8, dp_rows), F32),
+        sm_z=((NZ, 8, dp_rows), F32),
+        sm_all=((8, dp_rows), F32),
+    )
+    for letter, rows, cols in (("k", dp_rows, 2 * I), ("q", dp_rows, I), ("o", o_rows, D)):
+        name = "g" + letter
+        buffers[name] = ((2, NC, rows, cols), B16)
+        for tail in ("_recv", "_sum", "_quad"):
+            buffers[name + tail] = ((NC, rows, cols), B16)
+        for tail in ("_z", "_zr"):
+            buffers[name + tail] = ((NZ, rows // NZ, cols), B16)
+        buffers[name + "_f"] = ((rows // NZ, cols), B16)
+    same = dict(gk="gu", gu_sum="act", gd_sum="d_up", gk_sum="df_send", dq_send="o_send", d_lat="up")
+    for name in same:
+        del buffers[name]
+    names = list(ins) + list(outs) + list(buffers) + ["lsem", "ssem", "rsem", "msem", "dsem"]
+    geo = (S, R, Q, D, I, NC, NZ)
+
+    def body(*refs):
+        table = dict(zip(names, refs))
+        for name, base in same.items():
+            table[name] = table[base]
+        fused_kernel(geo, types.SimpleNamespace(**table))
+
+    got = pl.pallas_call(
+        body,
+        out_shape=[jax.ShapeDtypeStruct(s, d) for s, d in outs.values()],
+        in_specs=in_specs,
+        out_specs=[hbm] * len(outs),
+        scratch_shapes=[pltpu.VMEM(s, d) for s, d in buffers.values()]
+        + [DMA((28,)), DMA((120,)), DMA((120,)), DMA((2,)), DMA((4,))],
+        compiler_params=pltpu.CompilerParams(
+            collective_id=1, has_side_effects=True, vmem_limit_bytes=VMEM_BYTES
+        ),
+        name="resampler",
+    )(*ins.values())
+    out = types.SimpleNamespace(**dict(zip(outs, got)))
+    grad_up = jnp.transpose(out.gup, (1, 0, 2))
+    return (
+        out.latents_out.reshape(latents.shape),
+        out.media_grad.reshape(media.shape),
+        out.latent_grad.reshape(latents.shape),
+        *[out.gsmall[i] for i in range(6)],
+        out.gquery.reshape(wq.shape).astype(F32),
+        out.gkv.reshape(wkv.shape).astype(F32),
+        out.gout.reshape(wo.shape).astype(F32),
+        grad_up.reshape(wup.shape).astype(F32),
+        out.gdown.reshape(wdown.shape).astype(F32),
+    )
+
+
 def solution(mesh):
     rows4 = P(None, "dp", "lat", None)
     vec = P("dp")
     mat = P("dp", None)
+    n_dp, n_lat = mesh.shape["dp"], mesh.shape["lat"]
+    body = fused if n_dp == 2 * n_lat else shards
     return jax.shard_map(
-        functools.partial(shards, mesh.shape["dp"], mesh.shape["lat"]),
+        functools.partial(body, n_dp, n_lat),
         mesh=mesh,
         in_specs=(rows4, rows4, P(None, "dp"), rows4) + (vec,) * 6 + (mat,) * 5,
         out_specs=(rows4,) * 3 + (vec,) * 6 + (mat,) * 5,

time: 610 us -> 263 us (0.43)
  the two profiles are of different devices: /device:TPU:13 before, /device:TPU:0 now
where the time goes in v2:
time: 263 us; the launch traced here: 262 us
  Pallas kernels  239 us (91%)
  local copies, waits for them, and re-layouts  15.2 us (6%)
  other arithmetic  7.51 us (3%)
    pallas_call x1, Pallas kernels, fused(): pl.pallas_call(body, out_shape=[jax.ShapeDtypeStruct(s, d) for s, d in ou...  239 us
    unnamed x13, local copies, waits for them, and re-layouts  10.6 us

profile of v2, /device:TPU:0, one launch (start us, length us, event | category | flops | bytes accessed | tf_op | source)
XLA Modules:
  0.0 262.4 jit_solution(17916189415879107102)
XLA Ops:
  0.6 0.8 copy.30
  1.4 0.6 reshape.67.refs_9_
  2.0 0.8 stack.27
  2.8 0.6 pad_convert_fusion.refs_3_
  3.4 239.0 %resampler.1 = (bf16[128,1024]{1,0:T(8,128)(2,1)}, bf16[8,320,1024]{2,1,0:T(8,128)(2,1)}, bf16[128,1024]{1,0:T(8,128)(2,1)}, f32[8,128]{1,0:T(8,128)}, bf16[4,32...) custom-call(bf16[8,320,1024]{2,1,0:T(8,128)(2,1)} %bitcast.41, ...), custom_call_target="tpu_custom_call" | custom-call | tf_op jit(solution)/shard_map/resampler/pallas_call | solution.py:933
  242.4 0.0 copy-start.1
  242.4 1.4 slice_bitcast_fusion
  243.8 1.6 bitcast_convert_fusion.3
  245.5 1.6 bitcast_convert_fusion.2
  247.1 1.8 bitcast_convert_fusion.1
  248.9 0.0 copy-done.1
  248.9 0.2 convert_bitcast_fusion
  249.1 1.8 copy.31
  250.9 0.0 copy-start
  250.9 3.0 %copy.32 = f32[128,4096]{1,0:T(8,128)} copy(f32[128,4096]{0,1:T(8,128)} %bitcast.39) | data formatting | bytes 4194304
  253.9 0.0 copy-done
  253.9 0.0 copy-start.3
  253.9 1.6 bitcast_convert_fusion
  255.5 0.0 copy-done.3
  255.6 0.7 copy.36
  256.3 0.0 copy-start.2
  256.3 5.5 %copy.37 = bf16[4,2,320,1024]{3,2,1,0:T(8,128)(2,1)} copy(bf16[4,2,320,1024]{3,2,1,0:T(8,128)(2,1)} %bitcast.40) | data formatting | bytes 10485760
  261.7 0.0 copy-done.2
  261.7 0.7 copy.38
Async XLA Ops:
  242.4 6.5 %copy-start.1 = (bf16[4,128,1024]{2,1,0:T(8,128)(2,1)S(1)}, bf16[4,128,1024]{2,1,0:T(8,128)(2,1)}, u32[]{:S(2)}) copy-start(bf16[4,128,1024]{2,1,0:T(8,128)(2,1)} %get-tuple-element.30) | copy-start | bytes 3145732
  250.9 3.0 %copy-start = (bf16[4,128,1024]{2,1,0:T(8,128)(2,1)S(1)}, bf16[4,128,1024]{2,1,0:T(8,128)(2,1)}, u32[]{:S(2)}) copy-start(bf16[4,128,1024]{2,1,0:T(8,128)(2,1)} %get-tuple-element.31) | copy-start | bytes 3145732
  253.9 1.6 copy-start.3
  256.3 5.5 %copy-start.2 = (bf16[128,1024]{1,0:T(8,128)(2,1)S(1)}, bf16[128,1024]{1,0:T(8,128)(2,1)}, u32[]{:S(2)}) copy-start(bf16[128,1024]{1,0:T(8,128)(2,1)} %get-tuple-element.25) | copy-start | bytes 786436

commit v3 on v2

--- a/solution.py
+++ b/solution.py
@@ -256,6 +256,16 @@
     )
 
 
+NORM_EARLY = 3
+UP_EARLY = 4
+HOP1, HOP2 = 2, 4
+HOPS_ATT = ((1, 3), (6, 4))
+HOPS_KV = ((1, 5),)
+HOPS_Q = (6, 7)
+HOPS_MED = ((2, 8), (5, 9))
+MED_SPLIT = 4
+HOP_END = 10
+
 NT, NN, TN = (((1,), (1,)), ((), ())), (((1,), (0,)), ((), ())), (((0,), (0,)), ((), ()))
 
 
@@ -323,18 +333,43 @@
         copy.start()
         return copy
 
+    class Planned:
+        def __init__(self, make):
+            at = used[1]
+            used[1] += 1
+
+            def build():
+                src, dst, where = make()
+                return pltpu.make_async_remote_copy(
+                    src, dst, r.ssem.at[at], r.rsem.at[at], device_id=where, device_id_type=MESH
+                )
+
+            self.build = build
+
+        def start(self):
+            self.build().start()
+
+        def wait(self):
+            self.build().wait()
+
+        def wait_send(self):
+            self.build().wait_send()
+
+        def wait_recv(self):
+            self.build().wait_recv()
+
     class Spread:
-        def __init__(self, src_for, dst):
-            self.dst = dst
-            self.far = [remote(src_for(chip_to(k)), dst.at[me], dp=2 * chip_to(k) + core) for k in quads]
-            self.near = remote(src_for(chip), dst.at[me], dp=sib)
-            self.own = local(src_for(chip), dst.at[me])
+        def __init__(self, src_for, dst_at):
+            self.dst_at = dst_at
+            self.far = [remote(src_for(chip_to(k)), dst_at(me), dp=2 * chip_to(k) + core) for k in quads]
+            self.near = remote(src_for(chip), dst_at(me), dp=sib)
+            self.own = local(src_for(chip), dst_at(me))
 
         def forward(self):
             self.passed = []
             for k in quads:
                 self.far[k - 1].wait_recv()
-                slot = self.dst.at[2 * chip_from(k) + core]
+                slot = self.dst_at(2 * chip_from(k) + core)
                 self.passed.append(remote(slot, slot, dp=sib))
 
         def finish(self):
@@ -355,6 +390,73 @@
         for copy in copies:
             copy.wait()
 
+    class Meet:
+        def __init__(self, own, got, cross, out, root):
+            self.own, self.got, self.crossed, self.out, self.root = own, got, cross, out, root
+            peer = 3 - root
+            self.up = Planned(lambda: (own, got, {"lat": 1 + z // 2}))
+            self.over = Planned(lambda: (own, cross, {"lat": root}))
+            self.near = Planned(lambda: (own, out, {"lat": 3 * (root - 1)}))
+            self.back = Planned(lambda: (own, out, {"lat": peer}))
+            self.far = Planned(lambda: (out, out, {"lat": 3 * (peer - 1)}))
+            self.lsem = r.lsem.at[used[0]]
+            used[0] += 1
+
+        def send(self):
+            @pl.when(jnp.logical_or(z == 0, z == NZ - 1))
+            def _():
+                self.up.start()
+
+        def merge(self):
+            @pl.when(z == 3 - self.root)
+            def _():
+                self.up.wait_recv()
+                self.own[...] = (self.own[...].astype(F32) + self.got[...].astype(F32)).astype(B16)
+                self.over.start()
+
+        def total(self):
+            @pl.when(z == self.root)
+            def _():
+                self.up.wait_recv()
+                both = self.own[...].astype(F32) + self.got[...].astype(F32)
+                self.over.wait_recv()
+                self.own[...] = (both + self.crossed[...].astype(F32)).astype(B16)
+                self.near.start()
+                self.back.start()
+                pltpu.make_async_copy(self.own, self.out, self.lsem).start()
+
+        def relay(self):
+            @pl.when(z == 3 - self.root)
+            def _():
+                self.back.wait_recv()
+                self.far.start()
+
+        def finish(self):
+            root, peer = self.root, 3 - self.root
+
+            @pl.when(jnp.logical_or(z == 0, z == NZ - 1))
+            def _():
+                self.up.wait_send()
+
+            @pl.when(z == 3 * (root - 1))
+            def _():
+                self.near.wait_recv()
+
+            @pl.when(z == 3 * (peer - 1))
+            def _():
+                self.far.wait_recv()
+
+            @pl.when(z == peer)
+            def _():
+                self.over.wait_send()
+                self.far.wait_send()
+
+            @pl.when(z == root)
+            def _():
+                self.near.wait_send()
+                self.back.wait_send()
+                pltpu.make_async_copy(self.own, self.out, self.lsem).wait()
+
     barrier = pltpu.get_barrier_semaphore()
     for k in quads:
         pl.semaphore_signal(barrier, inc=1, device_id={"dp": 2 * chip_to(k) + core}, device_id_type=MESH)
@@ -363,8 +465,17 @@
         pl.semaphore_signal(barrier, inc=1, device_id={"lat": z_to(k)}, device_id_type=MESH)
     pl.semaphore_wait(barrier, NC - 1 + 1 + NZ - 1)
 
-    g_small = Spread(lambda _: r.small, r.small_all)
-    g_wq = Spread(lambda _: r.wq, r.wq_all)
+    def whole(ref):
+        return lambda _: ref
+
+    def rows_at(ref):
+        return lambda d: ref.at[d]
+
+    def cols_at(ref, at, size):
+        return lambda d: ref.at[d, :, at : at + size]
+
+    g_small = Spread(whole(r.small), rows_at(r.small_all))
+    g_wq = Spread(whole(r.wq), rows_at(r.wq_all))
     lat_in = local(r.lat, r.lat_v)
     cot_in = local(r.cot, r.cot4.at[chip])
     slots = r.med.shape[0]
@@ -383,14 +494,12 @@
             med_copy(s + slots).start()
 
     med_first()
-    g_wkv = Spread(lambda _: r.wkv, r.wkv_all)
-    g_wo = Spread(lambda _: r.wo, r.wo_all)
     g_small.forward()
     g_small.finish()
     params = r.params
     for d in range(2 * NC):
         span = D // (2 * NC)
-        params[:, d * span : (d + 1) * span] = r.small_all[d]
+        params[0:6, d * span : (d + 1) * span] = r.small_all[d].astype(F32)
 
     def param(i):
         return params[i : i + 1, :]
@@ -398,8 +507,6 @@
     lat_in.wait()
     unit, _ = centred(r.lat_v[...].astype(F32))
     r.latn[...] = (unit * param(2) + param(3)).astype(B16)
-    g_wq.forward()
-
     rb = 64
 
     def norm_sample(s, carry):
@@ -420,32 +527,45 @@
         med_next(s)
         return carry
 
+    early = NORM_EARLY
+    lax.fori_loop(0, early, norm_sample, 0)
+    g_wq.forward()
+    g_key = Spread(lambda _: r.wkv.at[:, 0:I], cols_at(r.wkv_all, 0, I))
     g_wq.finish()
     query = dot(r.latn[...], r.wq_all[...].reshape(D, I), NN) * 0.125
     r.q_all[z] = query.astype(B16).reshape(S, Q, I)
     q_out = to_planes(lambda _: r.q_all.at[z], r.q_all.at[z])
-    lax.fori_loop(0, S, norm_sample, 0)
+    lax.fori_loop(early, S, norm_sample, 0)
     med_first()
-    g_wkv.forward()
-    g_wo.forward()
-    g_wkv.finish()
+    g_key.forward()
+    g_val = Spread(lambda _: r.wkv.at[:, I : 2 * I], cols_at(r.wkv_all, I, I))
+    g_wo = Spread(whole(r.wo), rows_at(r.wo_all))
+    g_key.finish()
     span = r.wup_all.shape[2]
 
     def up_slice(k):
         return r.wup.at[:, pl.ds(pl.multiple_of(k * span, 128), span)]
 
+    def key_cols(s, carry):
+        rows = pl.ds(pl.multiple_of(s * KR, 16), KR)
+        r.KV[rows, 0:I] = dot(r.X[rows, :], r.wkv_all[:, :, 0:I].reshape(D, I), NN).astype(B16)
+        return carry
+
+    def value_cols(s, carry):
+        rows = pl.ds(pl.multiple_of(s * KR, 16), KR)
+        r.KV[rows, I : 2 * I] = dot(r.X[rows, :], r.wkv_all[:, :, I : 2 * I].reshape(D, I), NN).astype(B16)
+        return carry
+
+    lax.fori_loop(0, S, key_cols, 0)
+    g_val.forward()
+    g_val.finish()
     cot_in.wait()
     g_cot = to_quad(lambda _: r.cot, r.cot4.at[chip])
     g_down = remote(r.wdown, r.wdown2.at[core], dp=sib)
     g_down_own = local(r.wdown, r.wdown2.at[core])
-    g_up = Spread(up_slice, r.wup_all)
-
-    def keyval(s, carry):
-        rows = pl.ds(pl.multiple_of(s * KR, 16), KR)
-        r.KV[rows, :] = dot(r.X[rows, :], r.wkv_all[...].reshape(D, 2 * I), NN).astype(B16)
-        return carry
-
-    lax.fori_loop(0, S, keyval, 0)
+    g_up = Spread(up_slice, rows_at(r.wup_all))
+    lax.fori_loop(0, S, value_cols, 0)
+    g_wo.forward()
     g_wo.finish()
     wait_all(q_out)
 
@@ -473,36 +593,27 @@
         rows = pl.ds(pl.multiple_of(s * KR, 16), KR)
         raw = dot(r.KV[rows, g * W : (g + 1) * W], qbig, NT)
         row = lax.broadcasted_iota(jnp.int32, raw.shape, 0)
-        live = jnp.logical_or(row >= R, row + z * R < r.counts[s] * VIS)
+        live = jnp.logical_or(row >= R, row + z * R < r.counts[s // r.counts.shape[1], lax.rem(s, r.counts.shape[1])] * VIS)
         return jnp.where(live, raw, -1e30)
 
     def queries(s, g):
         return spread_heads(r.q_all[:, s, :, g * W : (g + 1) * W].reshape(NZ * Q, W))
-
-    def stats(s, carry):
-        for g in range(G):
-            score = scores(s, g, queries(s, g))
-            top = jnp.max(score, 0, keepdims=True)
-            total = jnp.sum(jnp.exp(score - top), 0, keepdims=True)
-            r.lse[z, pl.ds(s * G + g, 1), :] = top + jnp.log(total)
-        return carry
-
-    lax.fori_loop(0, S, stats, 0)
-    wait_all(to_planes(lambda _: r.lse.at[z], r.lse.at[z]))
-    every = r.lse[...]
-    top = jnp.max(every, 0)
-    r.lse_all[...] = top + jnp.log(jnp.sum(jnp.exp(every - top[None]), 0))
 
     def attend(s, carry):
         rows = pl.ds(pl.multiple_of(s * KR, 16), KR)
         for g in range(G):
             score = scores(s, g, queries(s, g))
-            prob = jnp.exp(score - r.lse_all[pl.ds(s * G + g, 1), :])
-            part = dot(prob.astype(B16), r.KV[rows, I + g * W : I + (g + 1) * W], TN)
+            top = jnp.max(score, 0, keepdims=True)
+            grown = jnp.exp(score - top)
+            total = jnp.sum(grown, 0, keepdims=True)
+            r.lse[z, pl.ds(g * S + s, 1), :] = top + jnp.log(total)
+            prob = (grown * (1.0 / total)).astype(B16)
+            part = dot(prob, r.KV[rows, I + g * W : I + (g + 1) * W], TN)
             r.o_send[:, s, :, g * W : (g + 1) * W] = take_heads(part).astype(B16).reshape(NZ, Q, W)
         return carry
 
     lax.fori_loop(0, S, attend, 0)
+    lse_out = to_planes(lambda _: r.lse.at[z], r.lse.at[z])
     o_out = to_planes(lambda k: r.o_send.at[k], r.o_recv.at[z])
     g_up.forward()
     wait_all(g_cot)
@@ -515,11 +626,33 @@
 
     lax.fori_loop(0, NC, act_grad, 0)
     g_up.finish()
+    wait_all(lse_out)
+    every = r.lse[...]
+    top = jnp.max(every, 0)
+    lse_all = top + jnp.log(jnp.sum(jnp.exp(every - top[None]), 0))
+    r.lse_all[...] = lse_all
+    r.lse[...] = jnp.exp(every - lse_all[None])
+    pick = (
+        lax.rem(lax.broadcasted_iota(jnp.int32, (B, HG * NZ * Q), 1), NZ * Q)
+        == lax.rem(lax.broadcasted_iota(jnp.int32, (B, HG * NZ * Q), 0), Q) + z * Q
+    )
+    for k in range(NZ):
+        store = r.hidden if k < 2 else r.d_hidden
+        for g in range(G):
+            lanes = jnp.broadcast_to(
+                r.lse[z_from(k), g * S : (g + 1) * S, :][:, None, :], (S, Q, HG * NZ * Q)
+            ).reshape(B, HG * NZ * Q)
+            lanes = jnp.where(pick, lanes, 0.0)
+            coarse = lanes.astype(B16)
+            fine = (lanes - coarse.astype(F32)).astype(B16)
+            at = (k % 2) * I + g * W
+            store[:, at : at + W] = dot(coarse, r.mask[...], NN) + dot(fine, r.mask[...], NN)
     wait_all(o_out)
-    att = r.o_send[z].astype(F32)
+    att = r.hidden[:, 0:I] * r.o_send[z].astype(F32).reshape(B, I)
     for k in planes:
-        att = att + r.o_recv[z_from(k)].astype(F32)
-    att = att.reshape(B, I)
+        store = r.hidden if k < 2 else r.d_hidden
+        at = (k % 2) * I
+        att = att + store[:, at : at + I] * r.o_recv[z_from(k)].astype(F32).reshape(B, I)
     r.att_f[...] = att
     r.att[...] = att.astype(B16)
     hidden = r.lat_v[...].astype(F32) + dot(r.att[...], r.wo_all[...].reshape(I, D), NN)
@@ -551,13 +684,6 @@
         feed(b)
         df_out.append(remote(r.df_send.at[b], r.df_recv.at[chip], dp=2 * b + core))
 
-    def down(i, carry):
-        r.out_send[i] = dot(r.act[i], r.wdown2[...].reshape(span, D), NN).astype(B16)
-        return carry
-
-    lax.fori_loop(0, NC, down, 0)
-    out_out = to_quad(lambda k: r.out_send.at[k], r.out_recv.at[chip])
-
     half = span // 2
     act2 = r.act
 
@@ -585,6 +711,47 @@
 
     lax.fori_loop(0, NC, grad_up, 0)
     gu_out = remote(r.gu.at[other], r.gu_recv, dp=sib)
+
+    def down(i, carry):
+        r.out_send[i] = dot(r.act[i], r.wdown2[...].reshape(span, D), NN).astype(B16)
+        return carry
+
+    lax.fori_loop(0, NC, down, 0)
+    piece = half // NZ
+    gd_out.wait()
+    for j in range(NZ):
+        rows = slice(j * piece, (j + 1) * piece)
+        r.gd_sum[j] = (r.gd[core, rows, :].astype(F32) + r.gd_recv[rows, :].astype(F32)).astype(B16)
+
+    meets = [
+        Meet(r.gd_sum.at[j], r.z_got.at[j], r.z_cross.at[j // 2], r.gdown.at[j * piece : (j + 1) * piece, :], 1 + j % 2)
+        for j in range(NZ)
+    ]
+    meets += [
+        Meet(r.gu_quad.at[j], r.z_got.at[NZ + j], r.z_cross.at[(NZ + j) // 2], r.gup.at[:, j * span : (j + 1) * span], 1 + j % 2)
+        for j in range(NC)
+    ]
+    for part_, got_, cross_, out_ in (
+        (r.go_t, r.go_got, r.go_cross, r.gout),
+        (r.gk_t, r.gk_got, r.gk_cross, r.gkv),
+        (r.gq_t, r.gq_got, r.gq_cross, r.gquery),
+    ):
+        rows = part_.shape[1]
+        meets += [
+            Meet(part_.at[j], got_.at[j], cross_, out_.at[j * rows : (j + 1) * rows, :], 1 + j) for j in range(2)
+        ]
+
+    def hop(n):
+        if 0 <= n < len(meets):
+            meets[n].merge()
+        if 0 <= n - HOP1 < len(meets):
+            meets[n - HOP1].total()
+        if 0 <= n - HOP2 < len(meets):
+            meets[n - HOP2].relay()
+
+    for n in range(UP_EARLY):
+        meets[n].send()
+    gu_out.wait()
 
     for copy in f_out:
         copy.wait_send()
@@ -623,13 +790,6 @@
         r.go[1, i] = value[oh:]
     go_out = remote(r.go.at[other], r.go_recv, dp=sib)
 
-    wait_all(out_out)
-    out = r.hidden[...] + r.out_send[chip].astype(F32)
-    for k in quads:
-        out = out + r.out_recv[chip_to(k)].astype(F32)
-    r.stage[0] = out.astype(B16)
-    put_out = local(r.stage.at[0], r.latents_out)
-
     def add_pair(dst, a, b, n):
         def body(i, carry):
             dst[i] = (a[i].astype(F32) + b[i].astype(F32)).astype(B16)
@@ -637,15 +797,38 @@
 
         lax.fori_loop(0, n, body, 0)
 
-    gd_out.wait()
-    piece = half // NZ
-    for j in range(NZ):
-        rows = slice(j * piece, (j + 1) * piece)
-        r.gd_sum[j] = (r.gd[core, rows, :].astype(F32) + r.gd_recv[rows, :].astype(F32)).astype(B16)
-    gz_out = to_planes(lambda k: r.gd_sum.at[k], r.gz_recv.at[0, z])
-    gu_out.wait()
     add_pair(r.gu_sum, r.gu.at[core], r.gu_recv, NC)
-    gq_out = to_quad(lambda k: r.gu_sum.at[k], r.gu_quad.at[chip])
+    guq_out = to_quad(lambda k: r.gu_sum.at[k], r.gu_quad.at[chip])
+    out_out = to_quad(lambda k: r.out_send.at[k], r.out_recv.at[chip])
+    go_out.wait()
+    add_pair(r.go_sum, r.go.at[core], r.go_recv, NC)
+    goq_out = to_quad(lambda k: r.go_sum.at[k], r.go_quad.at[chip])
+    for n in range(UP_EARLY, NZ):
+        meets[n].send()
+    hop(0)
+    hop(1)
+    wait_all(guq_out)
+    r.gu_quad[chip] = r.gu_sum[chip]
+    for n in range(NZ, NZ + NC):
+        meets[n].send()
+
+    def quad_total(own, got):
+        total = own[chip].astype(F32)
+        for k in quads:
+            total = total + got[chip_to(k)].astype(F32)
+        return total
+
+    def split_total(dst, own, got):
+        total = quad_total(own, got).astype(B16)
+        rows = total.shape[0] // 2
+        for j in range(2):
+            dst[j] = total[j * rows : (j + 1) * rows]
+
+    wait_all(goq_out)
+    split_total(r.go_t, r.go_sum, r.go_quad)
+    for n in (8, 9):
+        meets[n].send()
+    hop(2)
     wait_all(d_out)
 
     ones = jnp.ones((KR, 128), B16)
@@ -661,7 +844,7 @@
         for g in range(G):
             qbig = queries(s, g)
             score = scores(s, g, qbig)
-            prob = jnp.exp(score - r.lse_all[pl.ds(s * G + g, 1), :])
+            prob = jnp.exp(score - r.lse_all[pl.ds(g * S + s, 1), :])
             dbig = spread_heads(r.d_ext[:, s, :, g * W : (g + 1) * W].reshape(NZ * Q, W))
             minus = r.d_ext[:, s, :, I : I + 128].reshape(NZ * Q, 128)
             minus = jnp.concatenate([minus] * HG, 0) * r.mask_e[g]
@@ -671,20 +854,28 @@
             r.dq_send[:, s, :, g * W : (g + 1) * W] = take_heads(dq).astype(B16).reshape(NZ, Q, W)
             r.KV[rows, g * W : (g + 1) * W] = dot(d_score, qbig, NN).astype(B16)
             r.KV[rows, I + g * W : I + (g + 1) * W] = dot(prob.astype(B16), dbig, NN).astype(B16)
+        for at, n in HOPS_ATT:
+
+            @pl.when(s == at)
+            def _():
+                hop(n)
+
         return carry
 
     lax.fori_loop(0, S, attend_back, 0)
     dq_out = to_planes(lambda k: r.dq_send.at[k], r.dq_recv.at[z])
-
-    wait_all(gq_out)
-    r.gu_quad[chip] = r.gu_sum[chip]
-    gz_out += to_planes(lambda k: r.gu_quad.at[k], r.gz_recv.at[1, z])
 
     def grad_kv(i, carry):
         at = pl.multiple_of(i * dw, dw)
         value = dot(r.X[:, pl.ds(at, dw)], r.KV[...], TN).astype(B16)
         r.gk[0, i] = value[:hw]
         r.gk[1, i] = value[hw:]
+        for at, n in HOPS_KV:
+
+            @pl.when(i == at)
+            def _():
+                hop(n)
+
         return carry
 
     lax.fori_loop(0, NC, grad_kv, 0)
@@ -701,25 +892,13 @@
         r.gq[1, i] = value[hw:]
     gqs_out = remote(r.gq.at[other], r.gq_recv, dp=sib)
     gk_out.wait()
-    go_out.wait()
     add_pair(r.gk_sum, r.gk.at[core], r.gk_recv, NC)
-    add_pair(r.go_sum, r.go.at[core], r.go_recv, NC)
-    quad_out = to_quad(lambda k: r.gk_sum.at[k], r.gk_quad.at[chip])
-    quad_out += to_quad(lambda k: r.go_sum.at[k], r.go_quad.at[chip])
+    gkq_out = to_quad(lambda k: r.gk_sum.at[k], r.gk_quad.at[chip])
     gqs_out.wait()
     add_pair(r.gq_sum, r.gq.at[core], r.gq_recv, NC)
-    quad_out += to_quad(lambda k: r.gq_sum.at[k], r.gq_quad.at[chip])
-
-    wait_all(gz_out)
-    for a, own in enumerate([r.gd_sum, r.gu_quad]):
-        total = own[z].astype(F32)
-        for k in planes:
-            total = total + r.gz_recv[a, z_from(k)].astype(F32)
-        r.gz_sum[a] = total.astype(B16)
-    last = []
-    for a, out in enumerate([r.gdown, r.gup]):
-        last.append(local(r.gz_sum.at[a], out.at[z]))
-        last += to_planes(lambda _: r.gz_sum.at[a], out.at[z])
+    gqq_out = to_quad(lambda k: r.gq_sum.at[k], r.gq_quad.at[chip])
+    for n in HOPS_Q:
+        hop(n)
 
     sums[0:1, :] = jnp.zeros((1, D), F32)
     sums[1:2, :] = jnp.zeros((1, D), F32)
@@ -749,9 +928,22 @@
         lax.fori_loop(0, R // rb, part, 0)
         pltpu.make_async_copy(r.mg.at[slot], r.media_grad.at[s], r.msem.at[slot]).start()
         med_next(s)
+        for at, n in HOPS_MED:
+
+            @pl.when(s == at)
+            def _():
+                hop(n)
+
         return carry
 
-    lax.fori_loop(0, S, media_back, 0)
+    lax.fori_loop(0, MED_SPLIT, media_back, 0)
+    wait_all(gkq_out)
+    split_total(r.gk_t, r.gk_sum, r.gk_quad)
+    wait_all(gqq_out)
+    split_total(r.gq_t, r.gq_sum, r.gq_quad)
+    for n in range(10, 14):
+        meets[n].send()
+    lax.fori_loop(MED_SPLIT, S, media_back, 0)
 
     d_latn = r.d_lat[...] + dot(r.dq[...], r.wq_all[...].reshape(D, I), NT)
     unit, factor = centred(r.lat_v[...].astype(F32))
@@ -766,47 +958,35 @@
             d = 2 * t + cc
             r.sm[cc, t] = sums[:, d * sp : (d + 1) * sp]
     sm_out = remote(r.sm.at[other], r.sm_recv, dp=sib)
+    hop(HOP_END)
     sm_out.wait()
     r.sm_sum[...] = r.sm[core] + r.sm_recv[...]
-    quad_out += to_quad(lambda k: r.sm_sum.at[k], r.sm_quad.at[chip])
-    wait_all(quad_out)
-
-    def quad_total(own, got):
-        total = own[chip].astype(F32)
-        for k in quads:
-            total = total + got[chip_to(k)].astype(F32)
-        return total
-
+    smq_out = to_quad(lambda k: r.sm_sum.at[k], r.sm_quad.at[chip])
+    hop(HOP_END + 1)
+    wait_all(smq_out)
     r.sm_z[z] = quad_total(r.sm_sum, r.sm_quad)
     zs_out = to_planes(lambda _: r.sm_z.at[z], r.sm_z.at[z])
-    thirds = [
-        (r.gk_sum, r.gk_quad, r.gk_z, r.gk_zr, r.gk_f, r.gkv),
-        (r.gq_sum, r.gq_quad, r.gq_z, r.gq_zr, r.gq_f, r.gquery),
-        (r.go_sum, r.go_quad, r.go_z, r.go_zr, r.go_f, r.gout),
-    ]
-    for own, got, split, far, _, _ in thirds:
-        total = quad_total(own, got).astype(B16)
-        rows = total.shape[0] // NZ
-        for j in range(NZ):
-            split[j] = total[j * rows : (j + 1) * rows]
-        zs_out += to_planes(lambda k: split.at[k], far.at[z])
+    hop(HOP_END + 2)
+    wait_all(out_out)
+    out = r.hidden[...] + r.out_send[chip].astype(F32)
+    for k in quads:
+        out = out + r.out_recv[chip_to(k)].astype(F32)
+    r.stage[0] = out.astype(B16)
+    put_out = local(r.stage.at[0], r.latents_out)
+    for n in range(HOP_END + 3, len(meets) + HOP2):
+        hop(n)
     wait_all(zs_out)
     r.sm_all[...] = jnp.sum(r.sm_z[...], 0)
-    last.append(local(r.sm_all, r.gsmall))
-    for _, _, split, far, whole, out in thirds:
-        total = split[z].astype(F32)
-        for k in planes:
-            total = total + far[z_from(k)].astype(F32)
-        whole[...] = total.astype(B16)
-        last.append(local(whole, out.at[z]))
-        last += to_planes(lambda _: whole, out.at[z])
+    put_small = local(r.sm_all, r.gsmall)
+    for meet in meets:
+        meet.finish()
+    put_small.wait()
     for slot in range(2):
         pltpu.make_async_copy(
             r.mg.at[slot], r.media_grad.at[S - 2 + slot], r.msem.at[slot]
         ).wait()
     put_out.wait()
     put_lat.wait()
-    wait_all(last)
     assert used[1] <= r.rsem.shape[0] and used[0] <= r.lsem.shape[0]
 
 
@@ -821,8 +1001,7 @@
     KR = R + Q
     span = wup.shape[1] // NC
     dp_rows = D // n_dp
-    small = jnp.stack([g_m, b_m, g_l, b_l, g_f, b_f], 0).astype(F32)
-    small = jnp.pad(small, ((0, 2), (0, 0)))
+    small = jnp.stack([g_m, b_m, g_l, b_l, g_f, b_f], 0)
     hbm = pl.BlockSpec(memory_space=pl.ANY)
     ins = dict(
         media=media.reshape(S, R, D),
@@ -834,7 +1013,7 @@
         wo=wo,
         wup=wup,
         wdown=wdown,
-        counts=counts.reshape(S),
+        counts=counts,
     )
     in_specs = [hbm] * 9 + [pl.BlockSpec(memory_space=pltpu.SMEM)]
     outs = dict(
@@ -842,11 +1021,11 @@
         media_grad=((S, R, D), B16),
         latent_grad=((B, D), B16),
         gsmall=((8, dp_rows), F32),
-        gquery=((NZ, dp_rows // NZ, I), B16),
-        gkv=((NZ, dp_rows // NZ, 2 * I), B16),
-        gout=((NZ, I // n_dp // NZ, D), B16),
-        gup=((NC, dp_rows, span), B16),
-        gdown=((NZ, span // 2 // NZ, D), B16),
+        gquery=((dp_rows, I), B16),
+        gkv=((dp_rows, 2 * I), B16),
+        gout=((I // n_dp, D), B16),
+        gup=((dp_rows, NC * span), B16),
+        gdown=((span // 2, D), B16),
     )
     kv_rows = S * KR
     o_rows = I // n_dp
@@ -854,7 +1033,7 @@
         med=((4, R, D), B16),
         X=((kv_rows, D), B16),
         KV=((kv_rows, 2 * I), B16),
-        small_all=((n_dp, 8, dp_rows), F32),
+        small_all=((n_dp, 6, dp_rows), B16),
         params=((8, D), F32),
         wq_all=((n_dp, dp_rows, I), B16),
         wkv_all=((n_dp, dp_rows, 2 * I), B16),
@@ -890,8 +1069,8 @@
         gu_recv=((NC, dp_rows, span), B16),
         gu_sum=((NC, dp_rows, span), B16),
         gu_quad=((NC, dp_rows, span), B16),
-        gz_recv=((2, NZ, dp_rows, span), B16),
-        gz_sum=((2, dp_rows, span), B16),
+        z_got=((2 * NZ, dp_rows, span), B16),
+        z_cross=((NZ, dp_rows, span), B16),
         d_hidden=((B, D), F32),
         d_attn=((B, D), B16),
         d_ext=((NZ, S, Q, I + 128), B16),
@@ -915,9 +1094,9 @@
         buffers[name] = ((2, NC, rows, cols), B16)
         for tail in ("_recv", "_sum", "_quad"):
             buffers[name + tail] = ((NC, rows, cols), B16)
-        for tail in ("_z", "_zr"):
-            buffers[name + tail] = ((NZ, rows // NZ, cols), B16)
-        buffers[name + "_f"] = ((rows // NZ, cols), B16)
+        buffers[name + "_t"] = ((2, rows // 2, cols), B16)
+        buffers[name + "_got"] = ((2, rows // 2, cols), B16)
+        buffers[name + "_cross"] = ((rows // 2, cols), B16)
     same = dict(gk="gu", gu_sum="act", gd_sum="d_up", gk_sum="df_send", dq_send="o_send", d_lat="up")
     for name in same:
         del buffers[name]
@@ -936,25 +1115,101 @@
         in_specs=in_specs,
         out_specs=[hbm] * len(outs),
         scratch_shapes=[pltpu.VMEM(s, d) for s, d in buffers.values()]
-        + [DMA((28,)), DMA((120,)), DMA((120,)), DMA((2,)), DMA((4,))],
+        + [DMA((40,)), DMA((176,)), DMA((176,)), DMA((2,)), DMA((4,))],
         compiler_params=pltpu.CompilerParams(
             collective_id=1, has_side_effects=True, vmem_limit_bytes=VMEM_BYTES
         ),
         name="resampler",
     )(*ins.values())
-    out = types.SimpleNamespace(**dict(zip(outs, got)))
-    grad_up = jnp.transpose(out.gup, (1, 0, 2))
+    done = finish(got)
     return (
-        out.latents_out.reshape(latents.shape),
-        out.media_grad.reshape(media.shape),
-        out.latent_grad.reshape(latents.shape),
-        *[out.gsmall[i] for i in range(6)],
-        out.gquery.reshape(wq.shape).astype(F32),
-        out.gkv.reshape(wkv.shape).astype(F32),
-        out.gout.reshape(wo.shape).astype(F32),
-        grad_up.reshape(wup.shape).astype(F32),
-        out.gdown.reshape(wdown.shape).astype(F32),
+        done[0].reshape(latents.shape),
+        done[1].reshape(media.shape),
+        done[2].reshape(latents.shape),
+        *done[3:9],
+        *done[9:],
     )
+
+
+def finish_kernel(*refs):
+    ins, outs = refs[:9], refs[9:23]
+    stage, casts = refs[23:32], refs[32:37]
+    sem_in, sem_out = refs[37:]
+    parts = ins[1].shape[0]
+
+    def media(s, load):
+        if load:
+            return pltpu.make_async_copy(ins[1].at[s], stage[1].at[s], sem_in.at[9 + s])
+        return pltpu.make_async_copy(stage[1].at[s], outs[1].at[s], sem_out.at[9 + s])
+
+    loads = [pltpu.make_async_copy(ins[i], stage[i], sem_in.at[i]) for i in range(9) if i != 1]
+    order = [7, 6, 3, 4, 5, 0, 1, 2]
+    for s in range(parts // 2):
+        media(s, True).start()
+    for i in order[:2]:
+        loads[i].start()
+    for s in range(parts // 2, parts):
+        media(s, True).start()
+    for i in order[2:]:
+        loads[i].start()
+    for s in range(parts // 2):
+        media(s, True).wait()
+        media(s, False).start()
+    stores = []
+
+    def cast_one(i):
+        loads[3 + i].wait()
+        rows = stage[4 + i].shape[0]
+        step = 32
+
+        def cast(k, carry):
+            block = pl.ds(pl.multiple_of(k * step, step), step)
+            casts[i][block, :] = stage[4 + i][block, :].astype(F32)
+            return carry
+
+        lax.fori_loop(0, rows // step, cast, 0)
+        copy = pltpu.make_async_copy(casts[i], outs[9 + i], sem_out.at[3 + i])
+        copy.start()
+        stores.append(copy)
+
+    cast_one(4)
+    cast_one(3)
+    for s in range(parts // 2, parts):
+        media(s, True).wait()
+        media(s, False).start()
+    for i in range(3):
+        cast_one(i)
+    for at, i in enumerate((0, 2)):
+        loads[at].wait()
+        copy = pltpu.make_async_copy(stage[i], outs[i], sem_out.at[i])
+        copy.start()
+        stores.append(copy)
+    loads[2].wait()
+    for i in range(6):
+        outs[3 + i][...] = stage[3][i]
+    for s in range(parts):
+        media(s, False).wait()
+    for copy in stores:
+        copy.wait()
+
+
+def finish(got):
+    hbm = pl.BlockSpec(memory_space=pl.ANY)
+    vmem = pl.BlockSpec(memory_space=pltpu.VMEM)
+    shapes = [jax.ShapeDtypeStruct(x.shape, x.dtype) for x in got[:3]]
+    shapes += [jax.ShapeDtypeStruct((got[3].shape[1],), F32)] * 6
+    shapes += [jax.ShapeDtypeStruct(x.shape, F32) for x in got[4:]]
+    return pl.pallas_call(
+        finish_kernel,
+        out_shape=shapes,
+        in_specs=[hbm] * 9,
+        out_specs=[hbm] * 3 + [vmem] * 6 + [hbm] * 5,
+        scratch_shapes=[pltpu.VMEM(x.shape, x.dtype) for x in got]
+        + [pltpu.VMEM(x.shape, F32) for x in got[4:]]
+        + [DMA((9 + got[1].shape[0],))] * 2,
+        compiler_params=pltpu.CompilerParams(vmem_limit_bytes=VMEM_BYTES),
+        name="casts",
+    )(*got)
 
 
 def solution(mesh):
@@ -962,7 +1217,7 @@
     vec = P("dp")
     mat = P("dp", None)
     n_dp, n_lat = mesh.shape["dp"], mesh.shape["lat"]
-    body = fused if n_dp == 2 * n_lat else shards
+    body = fused if (n_dp, n_lat) == (8, 4) else shards
     return jax.shard_map(
         functools.partial(body, n_dp, n_lat),
         mesh=mesh,

time: 263 us -> 215 us (0.82)
  Pallas kernels: 239 us -> 211 us
  local copies, waits for them, and re-layouts: 15.2 us -> 2.67 us
  other arithmetic: 7.51 us -> 0 us
    pallas_call x1, Pallas kernels: 239 us -> 203 us  [fused(): pl.pallas_call(body, out_shape=[jax.ShapeDtypeStruct(s, d) for s, d in ou...]
    unnamed x13 -> x1, local copies, waits for them, and re-layouts: 10.6 us -> 1.34 us
    pallas_call x0 -> x1, Pallas kernels: none -> 7.95 us  [finish(): pl.pallas_call(finish_kernel, out_shape=shapes, in_specs=[hbm] * 9, out_s...]
    convert_element_type x5 -> x0, other arithmetic: 6.91 us -> none  [the longest x1 1.79 us: fused(): out.gkv.reshape(wkv.shape).astype(F32)]
where the time goes in v3:
time: 215 us; the launch traced here: 214 us
  Pallas kernels  211 us (98%)
  local copies, waits for them, and re-layouts  2.67 us (1%)
    pallas_call x1, Pallas kernels, fused(): pl.pallas_call(body, out_shape=[jax.ShapeDtypeStruct(s, d) for s, d in ou...  203 us
    pallas_call x1, Pallas kernels, finish(): pl.pallas_call(finish_kernel, out_shape=shapes, in_specs=[hbm] * 9, out_s...  7.95 us

profile of v3, /device:TPU:0, one launch (start us, length us, event | category | flops | bytes accessed | tf_op | source)
XLA Modules:
  0.0 214.3 jit_solution(13414475403581981945)
XLA Ops:
  0.6 1.3 copy.29.refs_9_
  2.0 1.3 stack.27.refs_3_
  3.3 202.8 %resampler.1 = (bf16[128,1024]{1,0:T(8,128)(2,1)}, bf16[8,320,1024]{2,1,0:T(8,128)(2,1)}, bf16[128,1024]{1,0:T(8,128)(2,1)}, f32[8,128]{1,0:T(8,128)}, bf16[128,...) custom-call(bf16[8,320,1024]{2,1,0:T(8,128)(2,1)} %bitcast.12, ...), custom_call_target="tpu_custom_call" | custom-call | tf_op jit(solution)/shard_map/resampler/pallas_call | solution.py:1112
  206.2 8.0 %casts.1 = (bf16[128,1024]{1,0:T(8,128)(2,1)}, bf16[8,320,1024]{2,1,0:T(8,128)(2,1)}, bf16[128,1024]{1,0:T(8,128)(2,1)}, f32[128]{0:T(128)}, f32[128]{0:T(128)},...) custom-call(bf16[128,1024]{1,0:T(8,128)(2,1)} %get-tuple-element.37., ...), custom_call_target="tpu_custom_call" | custom-call | tf_op jit(solution)/shard_map/casts/pallas_call | solution.py:1202

commit v4 on v3

--- a/solution.py
+++ b/solution.py
@@ -256,13 +256,16 @@
     )
 
 
-NORM_EARLY = 3
+ROWS_STEP = 160
+NORMS = (3, 6)
 UP_EARLY = 4
 HOP1, HOP2 = 2, 4
-HOPS_ATT = ((1, 3), (6, 4))
-HOPS_KV = ((1, 5),)
-HOPS_Q = (6, 7)
-HOPS_MED = ((2, 8), (5, 9))
+HOPS_DEXT = (0, 1)
+HOPS_MID = (2,)
+HOPS_ATT = ()
+HOPS_KV = ((1, 3), (3, 4))
+HOPS_Q = (5, 6)
+HOPS_MED = ((1, 7), (4, 8), (6, 9))
 MED_SPLIT = 4
 HOP_END = 10
 
@@ -380,6 +383,47 @@
             for copy in self.passed:
                 copy.wait()
 
+    side = chip + 1 - 2 * lax.rem(chip, 2)
+    ahead = chip + 2 - 4 * (chip // 2)
+    cross = 3 - chip
+
+    class Relay(Spread):
+        def __init__(self, src_for, dst_at):
+            self.dst_at = dst_at
+            self.own = local(src_for(chip), dst_at(me))
+            self.far = [remote(src_for(t), dst_at(me), dp=2 * t + core) for t in (side, ahead)]
+            self.near = remote(src_for(chip), dst_at(me), dp=sib)
+            self.half = dst_at(me).shape[0] // 2
+
+        def forward(self):
+            self.passed = []
+            h = self.half
+            for k, (source, target, at) in enumerate(((side, ahead, 0), (ahead, side, h))):
+                self.far[k].wait_recv()
+                slot = self.dst_at(2 * source + core)
+                part = slot.at[at : at + h]
+                self.passed.append(remote(part, part, dp=2 * target + core))
+                self.passed.append(remote(slot, slot, dp=sib))
+
+        def forward2(self):
+            h = self.half
+            self.late = []
+            slot = self.dst_at(2 * cross + core)
+            for k, at in ((0, 0), (2, h)):
+                self.passed[k].wait_recv()
+                part = slot.at[at : at + h]
+                self.late.append(remote(part, part, dp=sib))
+
+        def finish(self):
+            self.own.wait()
+            self.near.wait()
+            for copy in self.far:
+                copy.wait_send()
+            for k in (0, 2):
+                self.passed[k].wait_send()
+            for copy in (self.passed[1], self.passed[3], *self.late):
+                copy.wait()
+
     def to_quad(src_for, dst):
         return [remote(src_for(chip_to(k)), dst, dp=2 * chip_to(k) + core) for k in quads]
 
@@ -474,6 +518,21 @@
     def cols_at(ref, at, size):
         return lambda d: ref.at[d, :, at : at + size]
 
+    part_rows = D // (2 * NC)
+    per_slot = NC
+
+    def up_at(d):
+        at = pl.multiple_of(lax.rem(d, per_slot) * part_rows, part_rows)
+        return r.ffw.at[2 + d // per_slot, pl.ds(at, part_rows)]
+
+    span = r.wup.shape[1] // NC
+
+    def down_matrix():
+        return r.ffw[0:2].reshape(span, D)
+
+    def up_matrix():
+        return r.ffw[2:4].reshape(D, span)
+
     g_small = Spread(whole(r.small), rows_at(r.small_all))
     g_wq = Spread(whole(r.wq), rows_at(r.wq_all))
     lat_in = local(r.lat, r.lat_v)
@@ -498,8 +557,7 @@
     g_small.finish()
     params = r.params
     for d in range(2 * NC):
-        span = D // (2 * NC)
-        params[0:6, d * span : (d + 1) * span] = r.small_all[d].astype(F32)
+        params[0:6, d * part_rows : (d + 1) * part_rows] = r.small_all[d].astype(F32)
 
     def param(i):
         return params[i : i + 1, :]
@@ -507,7 +565,7 @@
     lat_in.wait()
     unit, _ = centred(r.lat_v[...].astype(F32))
     r.latn[...] = (unit * param(2) + param(3)).astype(B16)
-    rb = 64
+    rb = ROWS_STEP
 
     def norm_sample(s, carry):
         slot = lax.rem(s, slots)
@@ -527,46 +585,47 @@
         med_next(s)
         return carry
 
-    early = NORM_EARLY
-    lax.fori_loop(0, early, norm_sample, 0)
+    def up_slice(k):
+        return r.wup.at[:, pl.ds(pl.multiple_of(k * span, 128), span)]
+
+    def key_cols(s, carry):
+        rows = pl.ds(pl.multiple_of(s * KR, 16), KR)
+        r.KV[rows, 0:I] = dot(r.X[rows, :], r.wkv_all[:, :, 0:I].reshape(D, I), NN).astype(B16)
+        return carry
+
+    def value_cols(s, carry):
+        rows = pl.ds(pl.multiple_of(s * KR, 16), KR)
+        r.KV[rows, I : 2 * I] = dot(r.X[rows, :], r.wkv_all[:, :, I : 2 * I].reshape(D, I), NN).astype(B16)
+        return carry
+
+    first, second = NORMS
+    lax.fori_loop(0, first, norm_sample, 0)
+    g_key = Relay(lambda _: r.wkv.at[:, 0:I], cols_at(r.wkv_all, 0, I))
     g_wq.forward()
-    g_key = Spread(lambda _: r.wkv.at[:, 0:I], cols_at(r.wkv_all, 0, I))
+    g_val = Relay(lambda _: r.wkv.at[:, I : 2 * I], cols_at(r.wkv_all, I, I))
     g_wq.finish()
     query = dot(r.latn[...], r.wq_all[...].reshape(D, I), NN) * 0.125
     r.q_all[z] = query.astype(B16).reshape(S, Q, I)
     q_out = to_planes(lambda _: r.q_all.at[z], r.q_all.at[z])
-    lax.fori_loop(early, S, norm_sample, 0)
+    lax.fori_loop(first, second, norm_sample, 0)
+    g_key.forward()
+    g_wo = Relay(whole(r.wo), rows_at(r.wo_all))
+    lax.fori_loop(second, S, norm_sample, 0)
     med_first()
-    g_key.forward()
-    g_val = Spread(lambda _: r.wkv.at[:, I : 2 * I], cols_at(r.wkv_all, I, I))
-    g_wo = Spread(whole(r.wo), rows_at(r.wo_all))
+    g_key.forward2()
+    g_val.forward()
+    g_up = Spread(up_slice, up_at)
     g_key.finish()
-    span = r.wup_all.shape[2]
-
-    def up_slice(k):
-        return r.wup.at[:, pl.ds(pl.multiple_of(k * span, 128), span)]
-
-    def key_cols(s, carry):
-        rows = pl.ds(pl.multiple_of(s * KR, 16), KR)
-        r.KV[rows, 0:I] = dot(r.X[rows, :], r.wkv_all[:, :, 0:I].reshape(D, I), NN).astype(B16)
-        return carry
-
-    def value_cols(s, carry):
-        rows = pl.ds(pl.multiple_of(s * KR, 16), KR)
-        r.KV[rows, I : 2 * I] = dot(r.X[rows, :], r.wkv_all[:, :, I : 2 * I].reshape(D, I), NN).astype(B16)
-        return carry
-
     lax.fori_loop(0, S, key_cols, 0)
-    g_val.forward()
+    g_val.forward2()
+    g_wo.forward()
+    g_down = remote(r.wdown, r.ffw.at[core], dp=sib)
+    g_down_own = local(r.wdown, r.ffw.at[core])
     g_val.finish()
+    lax.fori_loop(0, S, value_cols, 0)
+    g_wo.forward2()
     cot_in.wait()
     g_cot = to_quad(lambda _: r.cot, r.cot4.at[chip])
-    g_down = remote(r.wdown, r.wdown2.at[core], dp=sib)
-    g_down_own = local(r.wdown, r.wdown2.at[core])
-    g_up = Spread(up_slice, rows_at(r.wup_all))
-    lax.fori_loop(0, S, value_cols, 0)
-    g_wo.forward()
-    g_wo.finish()
     wait_all(q_out)
 
     own_head = (
@@ -610,22 +669,25 @@
             prob = (grown * (1.0 / total)).astype(B16)
             part = dot(prob, r.KV[rows, I + g * W : I + (g + 1) * W], TN)
             r.o_send[:, s, :, g * W : (g + 1) * W] = take_heads(part).astype(B16).reshape(NZ, Q, W)
+
+        @pl.when(s == S // 2)
+        def _():
+            for copy in o_out[: NZ - 1]:
+                copy.start()
+
         return carry
 
+    def half(n):
+        return slice(n * (S // 2), (n + 1) * (S // 2))
+
+    def plan(make):
+        return [Planned(functools.partial(make, k, n)) for n in range(2) for k in planes]
+
+    o_out = plan(lambda k, n: (r.o_send.at[z_to(k), half(n)], r.o_recv.at[z, half(n)], {"lat": z_to(k)}))
     lax.fori_loop(0, S, attend, 0)
     lse_out = to_planes(lambda _: r.lse.at[z], r.lse.at[z])
-    o_out = to_planes(lambda k: r.o_send.at[k], r.o_recv.at[z])
-    g_up.forward()
-    wait_all(g_cot)
-    g_down.wait()
-    g_down_own.wait()
-
-    def act_grad(b, carry):
-        r.d_act[b] = dot(r.cot4[b], r.wdown2[...].reshape(span, D), NT)
-        return carry
-
-    lax.fori_loop(0, NC, act_grad, 0)
-    g_up.finish()
+    for copy in o_out[NZ - 1 :]:
+        copy.start()
     wait_all(lse_out)
     every = r.lse[...]
     top = jnp.max(every, 0)
@@ -647,6 +709,8 @@
             fine = (lanes - coarse.astype(F32)).astype(B16)
             at = (k % 2) * I + g * W
             store[:, at : at + W] = dot(coarse, r.mask[...], NN) + dot(fine, r.mask[...], NN)
+    g_up.forward()
+    g_wo.finish()
     wait_all(o_out)
     att = r.hidden[:, 0:I] * r.o_send[z].astype(F32).reshape(B, I)
     for k in planes:
@@ -661,8 +725,18 @@
     r.ffn4[chip] = (unit * param(4) + param(5)).astype(B16)
     f_out = to_quad(lambda _: r.ffn4.at[chip], r.ffn4.at[chip])
 
+    def act_grad(b, carry):
+        r.d_act[b] = dot(r.cot4[b], down_matrix(), NT)
+        return carry
+
+    wait_all(g_cot)
+    g_down.wait()
+    g_down_own.wait()
+    g_up.finish()
+    lax.fori_loop(0, NC, act_grad, 0)
+
     def feed(b):
-        r.up[...] = dot(r.ffn4[b], r.wup_all[...].reshape(D, span), NN)
+        r.up[...] = dot(r.ffn4[b], up_matrix(), NN)
 
         def gelu_part(i, carry):
             rows = pl.ds(pl.multiple_of(i * 32, 32), 32)
@@ -674,7 +748,7 @@
             return carry
 
         lax.fori_loop(0, B // 32, gelu_part, 0)
-        r.df_send[b] = dot(r.d_up[b], r.wup_all[...].reshape(D, span), NT).astype(B16)
+        r.df_send[b] = dot(r.d_up[b], up_matrix(), NT).astype(B16)
 
     feed(chip)
     df_out = []
@@ -684,7 +758,7 @@
         feed(b)
         df_out.append(remote(r.df_send.at[b], r.df_recv.at[chip], dp=2 * b + core))
 
-    half = span // 2
+    own_span = span // 2
     act2 = r.act
 
     def grad_down(i, carry):
@@ -692,7 +766,7 @@
         value = dot(
             act2[:, :, pl.ds(at, 256)].reshape(NC * B, 256), r.cot4[...].reshape(NC * B, D), TN
         )
-        r.gd[i // (half // 256), pl.ds(pl.multiple_of(lax.rem(i * 256, half), 256), 256), :] = value.astype(B16)
+        r.gd[i // (own_span // 256), pl.ds(pl.multiple_of(lax.rem(i * 256, own_span), 256), 256), :] = value.astype(B16)
         return carry
 
     lax.fori_loop(0, span // 256, grad_down, 0)
@@ -713,11 +787,11 @@
     gu_out = remote(r.gu.at[other], r.gu_recv, dp=sib)
 
     def down(i, carry):
-        r.out_send[i] = dot(r.act[i], r.wdown2[...].reshape(span, D), NN).astype(B16)
+        r.out_send[i] = dot(r.act[i], down_matrix(), NN).astype(B16)
         return carry
 
     lax.fori_loop(0, NC, down, 0)
-    piece = half // NZ
+    piece = own_span // NZ
     gd_out.wait()
     for j in range(NZ):
         rows = slice(j * piece, (j + 1) * piece)
@@ -780,7 +854,9 @@
     ext = jnp.where(lane < HEADS, coarse, delta - coarse).astype(B16)
     r.d_ext[z, :, :, 0:I] = d_att.reshape(S, Q, I)
     r.d_ext[z, :, :, I : I + 128] = ext.reshape(S, Q, 128)
-    d_out = to_planes(lambda _: r.d_ext.at[z], r.d_ext.at[z])
+    d_out = plan(lambda k, n: (r.d_ext.at[z, half(n)], r.d_ext.at[z, half(n)], {"lat": z_to(k)}))
+    for copy in d_out:
+        copy.start()
 
     ow = I // NC
     oh = ow // 2
@@ -799,18 +875,22 @@
 
     add_pair(r.gu_sum, r.gu.at[core], r.gu_recv, NC)
     guq_out = to_quad(lambda k: r.gu_sum.at[k], r.gu_quad.at[chip])
-    out_out = to_quad(lambda k: r.out_send.at[k], r.out_recv.at[chip])
+    for n in range(UP_EARLY, NZ):
+        meets[n].send()
+
+    def prob_at(s, g):
+        lanes = pl.ds(pl.multiple_of(lax.rem(s, 2) * I + g * W, W), W)
+        return r.ffw.at[s // 2, 0:KR, lanes]
+
+    def probs(s, carry):
+        for g in range(G):
+            score = scores(s, g, queries(s, g))
+            prob_at(s, g)[...] = jnp.exp(score - r.lse_all[pl.ds(g * S + s, 1), :]).astype(B16)
+        return carry
+
+    lax.fori_loop(0, S, probs, 0)
     go_out.wait()
     add_pair(r.go_sum, r.go.at[core], r.go_recv, NC)
-    goq_out = to_quad(lambda k: r.go_sum.at[k], r.go_quad.at[chip])
-    for n in range(UP_EARLY, NZ):
-        meets[n].send()
-    hop(0)
-    hop(1)
-    wait_all(guq_out)
-    r.gu_quad[chip] = r.gu_sum[chip]
-    for n in range(NZ, NZ + NC):
-        meets[n].send()
 
     def quad_total(own, got):
         total = own[chip].astype(F32)
@@ -824,12 +904,9 @@
         for j in range(2):
             dst[j] = total[j * rows : (j + 1) * rows]
 
-    wait_all(goq_out)
-    split_total(r.go_t, r.go_sum, r.go_quad)
-    for n in (8, 9):
-        meets[n].send()
-    hop(2)
-    wait_all(d_out)
+    for n in HOPS_DEXT:
+        hop(n)
+    wait_all(d_out[: NZ - 1])
 
     ones = jnp.ones((KR, 128), B16)
     lane_e = lax.broadcasted_iota(jnp.int32, (HG * NZ * Q, 128), 1)
@@ -839,37 +916,83 @@
             jnp.logical_or(lane_e == head_e + g * HG, lane_e == head_e + g * HG + HEADS).astype(F32).astype(B16)
         )
 
+    dq_out = plan(lambda k, n: (r.dq_send.at[z_to(k), half(n)], r.dq_recv.at[z, half(n)], {"lat": z_to(k)}))
+
     def attend_back(s, carry):
         rows = pl.ds(pl.multiple_of(s * KR, 16), KR)
+
         for g in range(G):
             qbig = queries(s, g)
-            score = scores(s, g, qbig)
-            prob = jnp.exp(score - r.lse_all[pl.ds(g * S + s, 1), :])
+            prob = prob_at(s, g)[...]
             dbig = spread_heads(r.d_ext[:, s, :, g * W : (g + 1) * W].reshape(NZ * Q, W))
             minus = r.d_ext[:, s, :, I : I + 128].reshape(NZ * Q, 128)
             minus = jnp.concatenate([minus] * HG, 0) * r.mask_e[g]
             d_prob = dot(r.KV[rows, I + g * W : I + (g + 1) * W], dbig, NT) + dot(ones, minus, NT)
-            d_score = (prob * d_prob).astype(B16)
+            d_score = (prob.astype(F32) * d_prob).astype(B16)
             dq = dot(d_score, r.KV[rows, g * W : (g + 1) * W], TN)
             r.dq_send[:, s, :, g * W : (g + 1) * W] = take_heads(dq).astype(B16).reshape(NZ, Q, W)
             r.KV[rows, g * W : (g + 1) * W] = dot(d_score, qbig, NN).astype(B16)
-            r.KV[rows, I + g * W : I + (g + 1) * W] = dot(prob.astype(B16), dbig, NN).astype(B16)
-        for at, n in HOPS_ATT:
-
-            @pl.when(s == at)
-            def _():
-                hop(n)
-
+            r.KV[rows, I + g * W : I + (g + 1) * W] = dot(prob, dbig, NN).astype(B16)
         return carry
 
-    lax.fori_loop(0, S, attend_back, 0)
-    dq_out = to_planes(lambda k: r.dq_send.at[k], r.dq_recv.at[z])
+    lax.fori_loop(0, S // 2, attend_back, 0)
+    for copy in dq_out[: NZ - 1]:
+        copy.start()
+    goq_out = to_quad(lambda k: r.go_sum.at[k], r.go_quad.at[chip])
+    out_out = to_quad(lambda k: r.out_send.at[k], r.out_recv.at[chip])
+    for n in HOPS_MID:
+        hop(n)
+    wait_all(d_out[NZ - 1 :])
+    lax.fori_loop(S // 2, S, attend_back, 0)
+    for copy in dq_out[NZ - 1 :]:
+        copy.start()
+    wait_all(guq_out)
+    r.gu_quad[chip] = r.gu_sum[chip]
+    for n in range(NZ, NZ + NC):
+        meets[n].send()
+    for n in HOPS_ATT:
+        hop(n)
+
+    def kv_chip(i):
+        return lax.rem(chip + 1 + i, NC)
+
+    def kv_pair(i):
+        return pltpu.make_async_remote_copy(
+            r.gk.at[other, kv_chip(i)],
+            r.gk_recv.at[kv_chip(i)],
+            r.ksem.at[0, i],
+            r.ksem.at[1, i],
+            device_id={"dp": sib},
+            device_id_type=MESH,
+        )
+
+    def kv_quad(i):
+        return pltpu.make_async_remote_copy(
+            r.gk_sum.at[kv_chip(i)],
+            r.gk_quad.at[chip],
+            r.ksem.at[2, i],
+            r.ksem.at[3, i],
+            device_id={"dp": 2 * kv_chip(i) + core},
+            device_id_type=MESH,
+        )
+
+    def kv_add(i):
+        kv_pair(i).wait()
+        b = kv_chip(i)
+        r.gk_sum[b] = (r.gk[core, b].astype(F32) + r.gk_recv[b].astype(F32)).astype(B16)
 
     def grad_kv(i, carry):
-        at = pl.multiple_of(i * dw, dw)
-        value = dot(r.X[:, pl.ds(at, dw)], r.KV[...], TN).astype(B16)
-        r.gk[0, i] = value[:hw]
-        r.gk[1, i] = value[hw:]
+        b = kv_chip(i)
+        value = dot(r.X[:, pl.ds(pl.multiple_of(b * dw, dw), dw)], r.KV[...], TN).astype(B16)
+        r.gk[0, b] = value[:hw]
+        r.gk[1, b] = value[hw:]
+        kv_pair(i).start()
+
+        @pl.when(i >= 1)
+        def _():
+            kv_add(i - 1)
+            kv_quad(i - 1).start()
+
         for at, n in HOPS_KV:
 
             @pl.when(i == at)
@@ -879,8 +1002,11 @@
         return carry
 
     lax.fori_loop(0, NC, grad_kv, 0)
-    gk_out = remote(r.gk.at[other], r.gk_recv, dp=sib)
-
+
+    wait_all(goq_out)
+    split_total(r.go_t, r.go_sum, r.go_quad)
+    for n in (8, 9):
+        meets[n].send()
     wait_all(dq_out)
     dq = r.dq_send[z].astype(F32)
     for k in planes:
@@ -891,9 +1017,7 @@
         r.gq[0, i] = value[:hw]
         r.gq[1, i] = value[hw:]
     gqs_out = remote(r.gq.at[other], r.gq_recv, dp=sib)
-    gk_out.wait()
-    add_pair(r.gk_sum, r.gk.at[core], r.gk_recv, NC)
-    gkq_out = to_quad(lambda k: r.gk_sum.at[k], r.gk_quad.at[chip])
+    kv_add(NC - 1)
     gqs_out.wait()
     add_pair(r.gq_sum, r.gq.at[core], r.gq_recv, NC)
     gqq_out = to_quad(lambda k: r.gq_sum.at[k], r.gq_quad.at[chip])
@@ -937,7 +1061,8 @@
         return carry
 
     lax.fori_loop(0, MED_SPLIT, media_back, 0)
-    wait_all(gkq_out)
+    for i in range(NC - 1):
+        kv_quad(i).wait()
     split_total(r.gk_t, r.gk_sum, r.gk_quad)
     wait_all(gqq_out)
     split_total(r.gq_t, r.gq_sum, r.gq_quad)
@@ -1038,8 +1163,7 @@
         wq_all=((n_dp, dp_rows, I), B16),
         wkv_all=((n_dp, dp_rows, 2 * I), B16),
         wo_all=((n_dp, o_rows, D), B16),
-        wup_all=((n_dp, dp_rows, span), B16),
-        wdown2=((2, span // 2, D), B16),
+        ffw=((4, span // 2, D), B16),
         lat_v=((B, D), B16),
         latn=((B, D), B16),
         cot4=((NC, B, D), B16),
@@ -1100,7 +1224,7 @@
     same = dict(gk="gu", gu_sum="act", gd_sum="d_up", gk_sum="df_send", dq_send="o_send", d_lat="up")
     for name in same:
         del buffers[name]
-    names = list(ins) + list(outs) + list(buffers) + ["lsem", "ssem", "rsem", "msem", "dsem"]
+    names = list(ins) + list(outs) + list(buffers) + ["lsem", "ssem", "rsem", "msem", "dsem", "ksem"]
     geo = (S, R, Q, D, I, NC, NZ)
 
     def body(*refs):
@@ -1115,7 +1239,7 @@
         in_specs=in_specs,
         out_specs=[hbm] * len(outs),
         scratch_shapes=[pltpu.VMEM(s, d) for s, d in buffers.values()]
-        + [DMA((40,)), DMA((176,)), DMA((176,)), DMA((2,)), DMA((4,))],
+        + [DMA((40,)), DMA((192,)), DMA((192,)), DMA((2,)), DMA((4,)), DMA((4, 4))],
         compiler_params=pltpu.CompilerParams(
             collective_id=1, has_side_effects=True, vmem_limit_bytes=VMEM_BYTES
         ),

time: 215 us -> 201 us (0.935)
  Pallas kernels: 211 us -> 197 us
    pallas_call x1, Pallas kernels: 203 us -> 189 us  [fused(): pl.pallas_call(body, out_shape=[jax.ShapeDtypeStruct(s, d) for s, d in ou...]
where the time goes in v4:
time: 201 us; the launch traced here: 200 us
  Pallas kernels  197 us (98%)
  local copies, waits for them, and re-layouts  2.67 us (1%)
    pallas_call x1, Pallas kernels, fused(): pl.pallas_call(body, out_shape=[jax.ShapeDtypeStruct(s, d) for s, d in ou...  189 us
    pallas_call x1, Pallas kernels, finish(): pl.pallas_call(finish_kernel, out_shape=shapes, in_specs=[hbm] * 9, out_s...  7.95 us

profile of v4, /device:TPU:0, one launch (start us, length us, event | category | flops | bytes accessed | tf_op | source)
XLA Modules:
  0.0 200.1 jit_solution(6161278414211873023)
XLA Ops:
  0.6 1.3 copy.29.refs_9_
  2.0 1.3 stack.27.refs_3_
  3.3 188.7 %resampler.1 = (bf16[128,1024]{1,0:T(8,128)(2,1)}, bf16[8,320,1024]{2,1,0:T(8,128)(2,1)}, bf16[128,1024]{1,0:T(8,128)(2,1)}, f32[8,128]{1,0:T(8,128)}, bf16[128,...) custom-call(bf16[8,320,1024]{2,1,0:T(8,128)(2,1)} %bitcast.12, ...), custom_call_target="tpu_custom_call" | custom-call | tf_op jit(solution)/shard_map/resampler/pallas_call | solution.py:1236
  192.0 8.0 %casts.1 = (bf16[128,1024]{1,0:T(8,128)(2,1)}, bf16[8,320,1024]{2,1,0:T(8,128)(2,1)}, bf16[128,1024]{1,0:T(8,128)(2,1)}, f32[128]{0:T(128)}, f32[128]{0:T(128)},...) custom-call(bf16[128,1024]{1,0:T(8,128)(2,1)} %get-tuple-element.37., ...), custom_call_target="tpu_custom_call" | custom-call | tf_op jit(solution)/shard_map/casts/pallas_call | solution.py:1326

commit v5 on v4

--- a/solution.py
+++ b/solution.py
@@ -256,9 +256,13 @@
     )
 
 
+PROB_SPLIT = 4
 ROWS_STEP = 160
 NORMS = (3, 6)
-UP_EARLY = 4
+SEND_A = (0, 1)
+SEND_B = (2, 3)
+SEND_C = ()
+SEND_D = ()
 HOP1, HOP2 = 2, 4
 HOPS_DEXT = (0, 1)
 HOPS_MID = (2,)
@@ -433,6 +437,41 @@
     def wait_all(copies):
         for copy in copies:
             copy.wait()
+
+    class Line:
+        def __init__(self, ref, part):
+            def flow(p, way):
+                return Planned(lambda: (ref.at[p, part], ref.at[p, part], {"lat": jnp.clip(z + way, 0, NZ - 1)}))
+
+            self.up = [flow(p, 1) for p in range(NZ - 1)]
+            self.down = [flow(p, -1) for p in range(1, NZ)]
+
+        def flows(self):
+            for p in range(NZ - 1):
+                yield p, 1, self.up[p]
+            for p in range(1, NZ):
+                yield p, -1, self.down[p - 1]
+
+        def send(self):
+            for p, _, copy in self.flows():
+                pl.when(z == p)(copy.start)
+
+        def step(self, far):
+            for p, way, copy in self.flows():
+                at = p + way * far
+                if 0 <= at < NZ:
+                    last = at == (NZ - 1 if way > 0 else 0)
+
+                    @pl.when(z == at)
+                    def _():
+                        copy.wait_recv()
+                        if not last:
+                            copy.start()
+
+        def finish(self):
+            for p, way, copy in self.flows():
+                sends = jnp.logical_and(z >= p, z < NZ - 1) if way > 0 else jnp.logical_and(z <= p, z > 0)
+                pl.when(sends)(copy.wait_send)
 
     class Meet:
         def __init__(self, own, got, cross, out, root):
@@ -761,16 +800,20 @@
     own_span = span // 2
     act2 = r.act
 
-    def grad_down(i, carry):
-        at = pl.multiple_of(i * 256, 256)
-        value = dot(
-            act2[:, :, pl.ds(at, 256)].reshape(NC * B, 256), r.cot4[...].reshape(NC * B, D), TN
-        )
-        r.gd[i // (own_span // 256), pl.ds(pl.multiple_of(lax.rem(i * 256, own_span), 256), 256), :] = value.astype(B16)
-        return carry
-
-    lax.fori_loop(0, span // 256, grad_down, 0)
+    def grad_down(half_core):
+        def body(i, carry):
+            at = pl.multiple_of(half_core * own_span + i * 256, 256)
+            value = dot(
+                act2[:, :, pl.ds(at, 256)].reshape(NC * B, 256), r.cot4[...].reshape(NC * B, D), TN
+            )
+            r.gd[half_core, pl.ds(pl.multiple_of(i * 256, 256), 256), :] = value.astype(B16)
+            return carry
+
+        lax.fori_loop(0, own_span // 256, body, 0)
+
+    grad_down(other)
     gd_out = remote(r.gd.at[other], r.gd_recv, dp=sib)
+    grad_down(core)
     dw = D // NC
     hw = dw // 2
 
@@ -786,11 +829,6 @@
     lax.fori_loop(0, NC, grad_up, 0)
     gu_out = remote(r.gu.at[other], r.gu_recv, dp=sib)
 
-    def down(i, carry):
-        r.out_send[i] = dot(r.act[i], down_matrix(), NN).astype(B16)
-        return carry
-
-    lax.fori_loop(0, NC, down, 0)
     piece = own_span // NZ
     gd_out.wait()
     for j in range(NZ):
@@ -823,8 +861,13 @@
         if 0 <= n - HOP2 < len(meets):
             meets[n - HOP2].relay()
 
-    for n in range(UP_EARLY):
+    for n in SEND_A:
         meets[n].send()
+    def down(i, carry):
+        r.out_send[i] = dot(r.act[i], down_matrix(), NN).astype(B16)
+        return carry
+
+    lax.fori_loop(0, NC, down, 0)
     gu_out.wait()
 
     for copy in f_out:
@@ -854,9 +897,9 @@
     ext = jnp.where(lane < HEADS, coarse, delta - coarse).astype(B16)
     r.d_ext[z, :, :, 0:I] = d_att.reshape(S, Q, I)
     r.d_ext[z, :, :, I : I + 128] = ext.reshape(S, Q, 128)
-    d_out = plan(lambda k, n: (r.d_ext.at[z, half(n)], r.d_ext.at[z, half(n)], {"lat": z_to(k)}))
-    for copy in d_out:
-        copy.start()
+    line = [Line(r.d_ext, half(n)) for n in range(2)]
+    for one in line:
+        one.send()
 
     ow = I // NC
     oh = ow // 2
@@ -875,7 +918,7 @@
 
     add_pair(r.gu_sum, r.gu.at[core], r.gu_recv, NC)
     guq_out = to_quad(lambda k: r.gu_sum.at[k], r.gu_quad.at[chip])
-    for n in range(UP_EARLY, NZ):
+    for n in SEND_B:
         meets[n].send()
 
     def prob_at(s, g):
@@ -888,7 +931,9 @@
             prob_at(s, g)[...] = jnp.exp(score - r.lse_all[pl.ds(g * S + s, 1), :]).astype(B16)
         return carry
 
-    lax.fori_loop(0, S, probs, 0)
+    lax.fori_loop(0, PROB_SPLIT, probs, 0)
+    line[0].step(1)
+    lax.fori_loop(PROB_SPLIT, S, probs, 0)
     go_out.wait()
     add_pair(r.go_sum, r.go.at[core], r.go_recv, NC)
 
@@ -904,9 +949,14 @@
         for j in range(2):
             dst[j] = total[j * rows : (j + 1) * rows]
 
+    line[0].step(2)
+    line[1].step(1)
     for n in HOPS_DEXT:
         hop(n)
-    wait_all(d_out[: NZ - 1])
+    line[0].step(3)
+    line[1].step(2)
+    for n in SEND_C:
+        meets[n].send()
 
     ones = jnp.ones((KR, 128), B16)
     lane_e = lax.broadcasted_iota(jnp.int32, (HG * NZ * Q, 128), 1)
@@ -942,8 +992,12 @@
     out_out = to_quad(lambda k: r.out_send.at[k], r.out_recv.at[chip])
     for n in HOPS_MID:
         hop(n)
-    wait_all(d_out[NZ - 1 :])
+    line[1].step(3)
+    for n in SEND_D:
+        meets[n].send()
     lax.fori_loop(S // 2, S, attend_back, 0)
+    for one in line:
+        one.finish()
     for copy in dq_out[NZ - 1 :]:
         copy.start()
     wait_all(guq_out)
@@ -1221,7 +1275,7 @@
         buffers[name + "_t"] = ((2, rows // 2, cols), B16)
         buffers[name + "_got"] = ((2, rows // 2, cols), B16)
         buffers[name + "_cross"] = ((rows // 2, cols), B16)
-    same = dict(gk="gu", gu_sum="act", gd_sum="d_up", gk_sum="df_send", dq_send="o_send", d_lat="up")
+    same = dict(gk="gu", gu_sum="act", gd_sum="d_up", gk_sum="df_send", dq_send="o_send", d_lat="up", stage="ffn4")
     for name in same:
         del buffers[name]
     names = list(ins) + list(outs) + list(buffers) + ["lsem", "ssem", "rsem", "msem", "dsem", "ksem"]

time: 201 us -> 192 us (0.955)
  Pallas kernels: 197 us -> 187 us
    pallas_call x1, Pallas kernels: 189 us -> 180 us  [fused(): pl.pallas_call(body, out_shape=[jax.ShapeDtypeStruct(s, d) for s, d in ou...]
where the time goes in v5:
time: 192 us; the launch traced here: 191 us
  Pallas kernels  187 us (97%)
  local copies, waits for them, and re-layouts  2.67 us (1%)
    pallas_call x1, Pallas kernels, fused(): pl.pallas_call(body, out_shape=[jax.ShapeDtypeStruct(s, d) for s, d in ou...  180 us
    pallas_call x1, Pallas kernels, finish(): pl.pallas_call(finish_kernel, out_shape=shapes, in_specs=[hbm] * 9, out_s...  7.95 us

profile of v5, /device:TPU:0, one launch (start us, length us, event | category | flops | bytes accessed | tf_op | source)
XLA Modules:
  0.0 190.9 jit_solution(16727303403771804430)
XLA Ops:
  0.6 1.3 copy.29.refs_9_
  2.0 1.3 stack.27.refs_3_
  3.3 179.5 %resampler.1 = (bf16[128,1024]{1,0:T(8,128)(2,1)}, bf16[8,320,1024]{2,1,0:T(8,128)(2,1)}, bf16[128,1024]{1,0:T(8,128)(2,1)}, f32[8,128]{1,0:T(8,128)}, bf16[128,...) custom-call(bf16[8,320,1024]{2,1,0:T(8,128)(2,1)} %bitcast.12, ...), custom_call_target="tpu_custom_call" | custom-call | tf_op jit(solution)/shard_map/resampler/pallas_call | solution.py:1290
  182.8 8.0 %casts.1 = (bf16[128,1024]{1,0:T(8,128)(2,1)}, bf16[8,320,1024]{2,1,0:T(8,128)(2,1)}, bf16[128,1024]{1,0:T(8,128)(2,1)}, f32[128]{0:T(128)}, f32[128]{0:T(128)},...) custom-call(bf16[128,1024]{1,0:T(8,128)(2,1)} %get-tuple-element.37., ...), custom_call_target="tpu_custom_call" | custom-call | tf_op jit(solution)/shard_map/casts/pallas_call | solution.py:1380

commit v6 on v5

--- a/solution.py
+++ b/solution.py
@@ -296,6 +296,7 @@
 def fused_kernel(geo, refs):
     S, R, Q, D, I, NC, NZ = geo
     KR = R + Q
+    per = refs.counts.shape[1]
     B = S * Q
     G = 2
     W = I // G
@@ -575,6 +576,7 @@
     g_small = Spread(whole(r.small), rows_at(r.small_all))
     g_wq = Spread(whole(r.wq), rows_at(r.wq_all))
     lat_in = local(r.lat, r.lat_v)
+    counts_in = local(r.counts, r.counts_s)
     cot_in = local(r.cot, r.cot4.at[chip])
     slots = r.med.shape[0]
 
@@ -665,6 +667,7 @@
     g_wo.forward2()
     cot_in.wait()
     g_cot = to_quad(lambda _: r.cot, r.cot4.at[chip])
+    counts_in.wait()
     wait_all(q_out)
 
     own_head = (
@@ -691,7 +694,7 @@
         rows = pl.ds(pl.multiple_of(s * KR, 16), KR)
         raw = dot(r.KV[rows, g * W : (g + 1) * W], qbig, NT)
         row = lax.broadcasted_iota(jnp.int32, raw.shape, 0)
-        live = jnp.logical_or(row >= R, row + z * R < r.counts[s // r.counts.shape[1], lax.rem(s, r.counts.shape[1])] * VIS)
+        live = jnp.logical_or(row >= R, row + z * R < r.counts_s[s // per, lax.rem(s, per)] * VIS)
         return jnp.where(live, raw, -1e30)
 
     def queries(s, g):
@@ -1122,6 +1125,12 @@
     split_total(r.gq_t, r.gq_sum, r.gq_quad)
     for n in range(10, 14):
         meets[n].send()
+    wait_all(out_out)
+    out = r.hidden[...] + r.out_send[chip].astype(F32)
+    for k in quads:
+        out = out + r.out_recv[chip_to(k)].astype(F32)
+    r.stage[0] = out.astype(B16)
+    put_out = local(r.stage.at[0], r.latents_out)
     lax.fori_loop(MED_SPLIT, S, media_back, 0)
 
     d_latn = r.d_lat[...] + dot(r.dq[...], r.wq_all[...].reshape(D, I), NT)
@@ -1146,12 +1155,6 @@
     r.sm_z[z] = quad_total(r.sm_sum, r.sm_quad)
     zs_out = to_planes(lambda _: r.sm_z.at[z], r.sm_z.at[z])
     hop(HOP_END + 2)
-    wait_all(out_out)
-    out = r.hidden[...] + r.out_send[chip].astype(F32)
-    for k in quads:
-        out = out + r.out_recv[chip_to(k)].astype(F32)
-    r.stage[0] = out.astype(B16)
-    put_out = local(r.stage.at[0], r.latents_out)
     for n in range(HOP_END + 3, len(meets) + HOP2):
         hop(n)
     wait_all(zs_out)
@@ -1194,7 +1197,7 @@
         wdown=wdown,
         counts=counts,
     )
-    in_specs = [hbm] * 9 + [pl.BlockSpec(memory_space=pltpu.SMEM)]
+    in_specs = [hbm] * 10
     outs = dict(
         latents_out=((B, D), B16),
         media_grad=((S, R, D), B16),
@@ -1278,7 +1281,7 @@
     same = dict(gk="gu", gu_sum="act", gd_sum="d_up", gk_sum="df_send", dq_send="o_send", d_lat="up", stage="ffn4")
     for name in same:
         del buffers[name]
-    names = list(ins) + list(outs) + list(buffers) + ["lsem", "ssem", "rsem", "msem", "dsem", "ksem"]
+    names = list(ins) + list(outs) + list(buffers) + ["lsem", "ssem", "rsem", "msem", "dsem", "ksem", "counts_s"]
     geo = (S, R, Q, D, I, NC, NZ)
 
     def body(*refs):
@@ -1293,7 +1296,7 @@
         in_specs=in_specs,
         out_specs=[hbm] * len(outs),
         scratch_shapes=[pltpu.VMEM(s, d) for s, d in buffers.values()]
-        + [DMA((40,)), DMA((192,)), DMA((192,)), DMA((2,)), DMA((4,)), DMA((4, 4))],
+        + [DMA((40,)), DMA((192,)), DMA((192,)), DMA((2,)), DMA((4,)), DMA((4, 4)), pltpu.SMEM(counts.shape, jnp.int32)],
         compiler_params=pltpu.CompilerParams(
             collective_id=1, has_side_effects=True, vmem_limit_bytes=VMEM_BYTES
         ),

time: 192 us -> 191 us (level)
  no operation moved by 1% of the time
where the time goes in v6:
time: 191 us; the launch traced here: 190 us
  Pallas kernels  187 us (98%)
  local copies, waits for them, and re-layouts  2.67 us (1%)
    pallas_call x1, Pallas kernels, fused(): pl.pallas_call(body, out_shape=[jax.ShapeDtypeStruct(s, d) for s, d in ou...  179 us
    pallas_call x1, Pallas kernels, finish(): pl.pallas_call(finish_kernel, out_shape=shapes, in_specs=[hbm] * 9, out_s...  7.95 us

profile of v6, /device:TPU:0, one launch (start us, length us, event | category | flops | bytes accessed | tf_op | source)
XLA Modules:
  0.0 190.3 jit_solution(12992383105585209497)
XLA Ops:
  0.6 1.3 copy.29.refs_9_
  2.0 1.3 stack.27.refs_3_
  3.3 178.9 %resampler.1 = (bf16[128,1024]{1,0:T(8,128)(2,1)}, bf16[8,320,1024]{2,1,0:T(8,128)(2,1)}, bf16[128,1024]{1,0:T(8,128)(2,1)}, f32[8,128]{1,0:T(8,128)}, bf16[128,...) custom-call(bf16[8,320,1024]{2,1,0:T(8,128)(2,1)} %bitcast.12, ...), custom_call_target="tpu_custom_call" | custom-call | tf_op jit(solution)/shard_map/resampler/pallas_call | solution.py:1293
  182.2 8.0 %casts.1 = (bf16[128,1024]{1,0:T(8,128)(2,1)}, bf16[8,320,1024]{2,1,0:T(8,128)(2,1)}, bf16[128,1024]{1,0:T(8,128)(2,1)}, f32[128]{0:T(128)}, f32[128]{0:T(128)},...) custom-call(bf16[128,1024]{1,0:T(8,128)(2,1)} %get-tuple-element.37., ...), custom_call_target="tpu_custom_call" | custom-call | tf_op jit(solution)/shard_map/casts/pallas_call | solution.py:1383
